TPU v7x, 32 devices: a whole 2x2x4 slice. The times are simulated.
32 devices in a mesh: tm: 8 (over z, y), order: 4 (over x, core).
Axes of the slice: x: 2, y: 2, z: 4, core: 2. Of those that a mesh axis runs over, the one named last changes fastest.
Arguments:
- design: bfloat16 [3, 1024, 65536], P(None, 'tm', 'order'), may hold values from -0.109375 to 0.109375
- gap_flags: int32 [1024], P('tm'), may hold values 0 or 1
- segment_ids: int32 [1024], P('tm'), may hold values from 0 to 3, never falling along the last dimension, each value on 1 to 512 neighbouring positions
- ar_order: int32 [3], replicated, may hold values from 1 to 4
- ma_order: int32 [3], replicated, may hold values from 1 to 4
- ar_roots: float32 [3, 4], replicated, may hold values from -0.5 to 1, as said below
- ma_roots: float32 [3, 4], replicated, may hold values from -0.5 to 1, as said below
- kaula: float32 [4, 16384], P('order', 'tm'), may hold values from 0.2 to 2
- precond: float32 [4, 128, 128, 128], P('order', 'tm'), as said below
- solution: float32 [16, 4, 16384], P(None, 'order', 'tm'), may hold values from -6 to 6
- residual: float32 [16, 4, 16384], P(None, 'order', 'tm'), may hold values from -6 to 6
- direction: float32 [16, 4, 16384], P(None, 'order', 'tm'), may hold values from -6 to 6
Outputs:
- new_solution: float32 [16, 4, 16384], P(None, 'order', 'tm')
- new_residual: float32 [16, 4, 16384], P(None, 'order', 'tm')
- new_direction: float32 [16, 4, 16384], P(None, 'order', 'tm')
Inputs may be any that keep to these rules, and one draw needn't show every extreme that they name: The first root of each component of ar_roots lies within 2 / 1024 below 1; the others lie within 0.5 of zero. The first root of each component of ma_roots lies within 12 / 1024 below 1; the others lie within 0.5 of zero. `precond`: every block is symmetric positive definite.
All inputs are finite; a program needn't handle non-finite values. No bound on the sum of `gap_flags` on one device may be relied on, other than what follows from the above.
Results may differ from a plain program's by a relative error of at most 0.0036.
Values may be sent and summed in bfloat16 or wider, within the bound.
A program may use at most 64 MiB of HBM per device.

v0:
```python
import functools

import jax
import jax.numpy as jnp
from jax import lax
from jax.experimental import pallas as pl
from jax.experimental.pallas import tpu as pltpu
from jax.sharding import PartitionSpec as P

LINK = jnp.bfloat16
LAGS = 4
HI = lax.Precision.HIGHEST
NN = (((1,), (0,)), ((), ()))
NT = (((1,), (1,)), ((), ()))


def dot(a, b, dims, precision=None):
    return lax.dot_general(a, b, dims, precision=precision, preferred_element_type=jnp.float32)


def rows_of(pieces, count, width):
    row = lax.broadcasted_iota(jnp.int32, (count, width), 0)
    out = jnp.zeros((count, width), jnp.float32)
    for at, piece in pieces:
        out = jnp.where(row == at, piece, out)
    return out


def tall(block, rows):
    return jnp.concatenate(
        [block, jnp.zeros((rows - block.shape[0], block.shape[1]), jnp.float32)], axis=0
    )


def bands(matrix):
    row = lax.broadcasted_iota(jnp.int32, matrix.shape, 0)
    col = lax.broadcasted_iota(jnp.int32, matrix.shape, 1)
    inside = row // LAGS == col // LAGS
    return [
        jnp.sum(
            jnp.where(inside & (row == col - shift), matrix, 0.0), axis=0, keepdims=True
        )
        for shift in range(1 - LAGS, LAGS)
    ]


def banded(vector, coeffs):
    width = vector.shape[1]
    total = None
    for shift, coeff in zip(range(1 - LAGS, LAGS), coeffs):
        moved = vector if shift == 0 else pltpu.roll(vector, shift % width, 1)
        total = moved * coeff if total is None else total + moved * coeff
    return total


def filters(ar_ref, ma_ref, aro_ref, mao_ref, ids, pt_ref):
    n = ids.shape[1]
    lane = lax.broadcasted_iota(jnp.int32, (1, n), 1)

    def lagged(v, k):
        return v if k == 0 else jnp.where(lane >= k, pltpu.roll(v, k, 1), 0.0)

    impulse = jnp.where(lane == 0, 1.0, 0.0).astype(jnp.float32)
    grid = jnp.broadcast_to(ids, (n, n))
    row = lax.broadcasted_iota(jnp.int32, (n, n), 0)
    col = lax.broadcasted_iota(jnp.int32, (n, n), 1)
    joined = (grid == grid.T) & (col >= row)
    out_rows, in_rows, end_rows = [], [], []
    for c in range(3):
        ar = [jnp.where(k < aro_ref[c], ar_ref[c, k], 0.0) for k in range(LAGS)]
        ma = [jnp.where(k < mao_ref[c], ma_ref[c, k], 0.0) for k in range(LAGS)]
        a, b = [1.0] + [0.0] * LAGS, [1.0] + [0.0] * LAGS
        for k in range(LAGS):
            a = [a[0]] + [a[j] - ar[k] * a[j - 1] for j in range(1, LAGS + 1)]
            b = [b[0]] + [b[j] - ma[k] * b[j - 1] for j in range(1, LAGS + 1)]
        h = impulse
        for k in range(LAGS):
            power, m = ar[k], 1
            while m < n:
                h = h + power * lagged(h, m)
                power, m = power * power, 2 * m
        g = h
        for k in range(LAGS):
            g = g - ma[k] * lagged(g, 1)
        for i in range(1, LAGS + 1):
            out_rows.append((c * LAGS + i - 1, lagged(h, i - 1)))
            acc = jnp.zeros_like(g)
            end = jnp.zeros_like(g)
            for m in range(LAGS + 1 - i):
                acc = acc + b[i + m] * lagged(impulse, m) - a[i + m] * lagged(g, m)
                end = end - a[i + m] * jnp.where(lane == n - 1 - m, 1.0, 0.0)
            in_rows.append((c * LAGS + i - 1, acc))
            end_rows.append((c * LAGS + i - 1, end))
        t = jnp.broadcast_to(g, (n, n))
        bit = 1
        while bit < n:
            t = jnp.where((row // bit) % 2 == 1, pltpu.roll(t, bit, 1), t)
            bit *= 2
        pt_ref[c] = jnp.where(joined, t, 0.0)
        yield None
    ca = rows_of(out_rows, 16, n)
    flip = jnp.where(row + col == n - 1, 1.0, 0.0).astype(jnp.float32)
    ab = dot(rows_of(in_rows, 16, n), flip, NN, HI)
    ends = rows_of(end_rows, 16, n)
    fwd = bands(dot(ca, tall(ends, n), NT, HI))
    bwd = bands(dot(ends, tall(ca, n), NT, HI))
    yield ca, ab, fwd, bwd


def spread(block, mask):
    row = lax.broadcasted_iota(jnp.int32, block.shape, 0)
    return jnp.concatenate(
        [jnp.where(row // LAGS == c, block * mask, 0.0) for c in range(3)], axis=1
    )

def kernel(
    T, O,
    design, ids_in, gaps_in, ar_ref, ma_ref, aro_ref, mao_ref, kaula, precond_in,
    res_in, direc_in,
    image_out, comb_out, scal_out,
    dv, precond, res, direc, packed, high, low,
    right_in, left_in, obs_out, obs_in, ids_all, summ_out, summ_in, pt,
    rs_right_out, rs_left_out, rs_right_in, rs_left_in, applied, image_applied,
    tot_out, tot_in, tot2_out, tot2_in,
    dsem, in_sem, agr_s, agr_r, agl_s, agl_r, ob_s, ob_r, id_s, id_r, su_s, su_r,
    rr_s, rr_r, rl_s, rl_r, t1_s, t1_r, t2_s, t2_r,
):
    me, order = lax.axis_index("tm"), lax.axis_index("order")
    A = T // 2
    rhs, share = packed.shape
    n = ids_in.shape[1]
    blocks = precond.shape[0]

    slow, fast = me // 2, me % 2
    partner = {"tm": 2 * slow + 1 - fast}

    def at_slow(k, other=0):
        row = 1 - fast if other else fast
        return 2 * lax.rem(slow + k + A, A) + row

    mesh_ids = pl.DeviceIdType.MESH

    def to_tm(k):
        return {"tm": lax.rem(me + k, T)}

    def to_order(k):
        return {"order": lax.rem(order + k, O)}

    def load(k, other):
        q = at_slow(k, other)
        slot = other * A + k % A
        return pltpu.make_async_copy(
            design.at[:, pl.ds(pl.multiple_of(q * share, 128), share)],
            dv.at[slot],
            dsem.at[slot],
        )

    def remote(src, dst, ssem, rsem, to):
        return pltpu.make_async_remote_copy(
            src_ref=src, dst_ref=dst, send_sem=ssem, recv_sem=rsem,
            device_id=to, device_id_type=mesh_ids,
        )

    get_direc = pltpu.make_async_copy(direc_in.at[:, 0, :], direc, in_sem.at[0])
    get_res = pltpu.make_async_copy(res_in.at[:, 0, :], res, in_sem.at[1])
    get_precond = pltpu.make_async_copy(precond_in, precond, in_sem.at[2])
    get_direc.start()
    barrier = pltpu.get_barrier_semaphore()
    for k in range(1, T):
        pl.semaphore_signal(barrier, inc=1, device_id=to_tm(k), device_id_type=mesh_ids)
    for k in range(1, O):
        pl.semaphore_signal(barrier, inc=1, device_id=to_order(k), device_id_type=mesh_ids)
    load(0, 0).start()
    get_precond.start()
    get_res.start()
    load(0, 1).start()
    for k in range(1, A):
        load(-k, 0).start()
        load(-k, 1).start()
    get_direc.wait()
    packed[...] = direc[...].astype(jnp.bfloat16)
    pl.semaphore_wait(barrier, T - 1 + O - 1)

    across = [remote(packed, right_in.at[k], agr_s.at[k], agr_r.at[k], {"tm": at_slow(k)})
              for k in range(1, A)]
    beside = [remote(packed, left_in.at[0], agl_s.at[0], agl_r.at[0], partner)]
    beside += [remote(right_in.at[k], left_in.at[k], agl_s.at[k], agl_r.at[k], partner)
               for k in range(1, A)]
    for copy in across + beside[:1]:
        copy.start()
    id_copies = [
        remote(ids_in, ids_all.at[k - 1], id_s.at[k - 1], id_r.at[k - 1], to_tm(k))
        for k in range(1, T)
    ]
    for copy in id_copies:
        copy.start()

    load(0, 0).wait()
    obs = dot(packed[...], dv[0], NT)
    ids = ids_in[0:1, :].astype(jnp.float32)
    building = filters(ar_ref, ma_ref, aro_ref, mao_ref, ids, pt)
    for k in range(1, A):
        across[k - 1].wait_recv()
        beside[k].start()
        if k == 1:
            beside[0].wait_recv()
            load(0, 1).wait()
            obs = obs + dot(left_in[0], dv[A], NT)
        load(-k, 0).wait()
        obs = obs + dot(right_in[k], dv[(-k) % A], NT)
        if k > 1:
            beside[k - 1].wait_recv()
            load(1 - k, 1).wait()
            obs = obs + dot(left_in[k - 1], dv[A + (1 - k) % A], NT)
        if k <= 3:
            next(building)
    for _ in range(3 - min(3, A - 1)):
        next(building)
    beside[A - 1].wait_recv()
    load(1 - A, 1).wait()
    obs = obs + dot(left_in[A - 1], dv[A + (1 - A) % A], NT)
    obs_out[...] = obs
    ob_copies = [
        remote(obs_out, obs_in.at[k - 1], ob_s.at[k - 1], ob_r.at[k - 1], to_order(k))
        for k in range(1, O)
    ]
    for copy in ob_copies:
        copy.start()

    ca, ab, fwd, bwd = next(building)
    first, last = ids[:, 0:1], ids[:, n - 1 : n]
    at_first = jnp.where(ids == first, 1.0, 0.0)
    at_last = jnp.where(ids == last, 1.0, 0.0)
    head_map = spread(ca, at_first)
    tail_map = spread(ab, at_last)
    head_map = jnp.concatenate(
        [dot(head_map[:, c * n : (c + 1) * n], pt[c], NT, HI) for c in range(3)], axis=1
    )
    state_map = jnp.concatenate([tall(tail_map, n // 2), tall(head_map, n // 2)], axis=0)
    for copy in id_copies:
        copy.wait_recv()
    ids_e = []
    for e in range(T):
        slot = jnp.minimum(lax.rem(me - e + T - 1, T), T - 2)
        ids_e.append(jnp.where(me == e, ids, ids_all[slot].astype(jnp.float32)))
    firsts = [v[:, 0:1] for v in ids_e]
    lasts = [v[:, n - 1 : n] for v in ids_e]
    runs = jnp.concatenate(
        [ca * jnp.where(v == f, 1.0, 0.0) for v, f in zip(ids_e, firsts)], axis=0
    )
    energy = dot(runs, tall(ca, n), NT, HI)
    energies = [bands(energy[16 * e : 16 * e + 16]) for e in range(T)]

    for copy in ob_copies:
        copy.wait_recv()
    for k in range(1, O):
        obs = obs + obs_in[k - 1]
    gaps3 = jnp.concatenate([gaps_in[0:1, :].astype(jnp.float32)] * 3, axis=1)
    masked = obs * gaps3
    summary = dot(masked, state_map, NT, HI)
    half = rhs // 2
    summ_out[...] = summary[:half] + pltpu.roll(summary[half:], 2 * 16, 1)
    su_copies = [
        remote(summ_out, summ_in.at[k - 1], su_s.at[k - 1], su_r.at[k - 1], to_tm(k))
        for k in range(1, T)
    ]
    for copy in su_copies:
        copy.start()
    local_back = jnp.concatenate(
        [
            dot(dot(masked[:, c * n : (c + 1) * n], pt[c], NN, HI), pt[c], NT, HI)
            for c in range(3)
        ],
        axis=1,
    )

    def preconditioned(v, cols):
        out = []
        for m in range(cols.start // 128, cols.stop // 128):
            x = v[:, m * 128 - cols.start : (m + 1) * 128 - cols.start]
            top = x.astype(jnp.bfloat16)
            rest = (x - top.astype(jnp.float32)).astype(jnp.bfloat16)
            both = dot(jnp.concatenate([top, rest], axis=0), high[m], NT)
            out.append(both[:rhs] + both[rhs:] + dot(top, low[m], NT))
        return jnp.concatenate(out, axis=1)

    get_precond.wait()
    for m in range(blocks):
        whole = precond[m]
        top = whole.astype(jnp.bfloat16)
        high[m] = top
        low[m] = (whole - top.astype(jnp.float32)).astype(jnp.bfloat16)
    get_res.wait()
    applied[...] = preconditioned(res[...], slice(0, share))
    for copy in su_copies:
        copy.wait_recv()
    sums = []
    for e in range(T):
        slot = jnp.minimum(lax.rem(me - e + T - 1, T), T - 2)
        got = summ_in[slot]
        got = jnp.concatenate([got, pltpu.roll(got, n - 2 * 16, 1)], axis=0)
        sums.append(jnp.where(me == e, summary, got))
    state = jnp.zeros_like(summary)
    mine_in = jnp.zeros_like(summary)
    ins = []
    for e in range(T):
        entering = state if e == 0 else state * jnp.where(lasts[e - 1] == firsts[e], 1.0, 0.0)
        ins.append(entering)
        mine_in = jnp.where(me == e, entering, mine_in)
        through = jnp.where(firsts[e] == lasts[e], 1.0, 0.0)
        state = sums[e] + through * banded(entering, fwd)
    back = jnp.zeros_like(summary)
    mine_back = jnp.zeros_like(summary)
    for e in range(T - 1, 0, -1):
        through = jnp.where(firsts[e] == lasts[e], 1.0, 0.0)
        heads = pltpu.roll(sums[e], n // 2, 1) + banded(ins[e], energies[e])
        back = (heads + through * banded(back, bwd)) * jnp.where(
            lasts[e - 1] == firsts[e], 1.0, 0.0
        )
        mine_back = jnp.where(me == e - 1, back, mine_back)
    lane = lax.broadcasted_iota(jnp.int32, summary.shape, 1)
    states = jnp.where(lane < n // 2, mine_back, pltpu.roll(mine_in, n // 2, 1))
    adjoint = local_back + dot(states, state_map, NN, HI)
    weighted = (adjoint * gaps3).astype(jnp.bfloat16)

    def grad(k, other):
        return dot(weighted, dv[other * A + k % A], NN)

    pair = [remote(rs_left_out.at[k], rs_left_in.at[k], rl_s.at[k], rl_r.at[k], partner)
            for k in range(A)]
    far = [remote(rs_right_out.at[k], rs_right_in.at[k], rr_s.at[k], rr_r.at[k],
                  {"tm": at_slow(k)}) for k in range(1, A)]
    order_of = list(range(1, A)) + [0]
    for k in order_of:
        rs_left_out[k] = grad(k, 1).astype(LINK)
        pair[k].start()
    for k in order_of[:-1]:
        piece = grad(k, 0)
        pair[k].wait_recv()
        rs_right_out[k] = (piece + rs_left_in[k].astype(jnp.float32)).astype(LINK)
        far[k - 1].start()
    image = grad(0, 0) + kaula[...] * direc[...]
    pair[0].wait_recv()
    image = image + rs_left_in[0].astype(jnp.float32)
    for k in order_of[:-1]:
        far[k - 1].wait_recv()
        image = image + rs_right_in[k].astype(jnp.float32)
    image_applied[...] = preconditioned(image, slice(0, share))
    image_out[...] = image
    app, imapp = applied[...], image_applied[...]
    d, r = direc[...], res[...]
    lane = lax.broadcasted_iota(jnp.int32, (rhs, 128), 1)
    row = lax.broadcasted_iota(jnp.int32, (rhs, 128), 0)
    products = [r * app, d * image, image * app, image * imapp]
    total = jnp.zeros((rhs, 128), jnp.float32)
    for q, product in enumerate(products):
        total = jnp.where(lane == q * rhs + row, jnp.sum(product, axis=1, keepdims=True), total)
    total = jnp.sum(total, axis=0, keepdims=True)

    def gather_sum(value, out, into, ssem, rsem, count, to):
        out[...] = value
        copies = [
            remote(out, into.at[k - 1], ssem.at[k - 1], rsem.at[k - 1], to(k))
            for k in range(1, count)
        ]
        for copy in copies:
            copy.start()
        for k, copy in enumerate(copies):
            copy.wait_recv()
            value = value + into[k]
        return value, copies

    total, c1 = gather_sum(total, tot_out, tot_in, t1_s, t1_r, O, to_order)
    total, c2 = gather_sum(total, tot2_out, tot2_in, t2_s, t2_r, T, to_tm)
    wide = jnp.broadcast_to(total[0:1, :], (rhs, 128))
    old_rz, curvature, cross, quad = [
        jnp.sum(jnp.where(lane == q * rhs + row, wide, 0.0), axis=1, keepdims=True)
        for q in range(4)
    ]
    step = old_rz / curvature
    new_rz = old_rz - 2.0 * step * cross + step * step * quad
    comb_out[...] = app - step * imapp
    scal_out[...] = jnp.where(lane == 0, step, new_rz / old_rz)

    for copy in across + beside + pair + far:
        copy.wait_send()
    for copy in id_copies + ob_copies + su_copies + c1 + c2:
        copy.wait_send()


def finish(image, comb, scal, sol, res, direc, new_sol, new_res, new_dir, got, put, isem, osem):
    def fetch(k, ref):
        return pltpu.make_async_copy(ref.at[:, 0, :], got.at[k], isem.at[k])

    def store(k, ref):
        return pltpu.make_async_copy(put.at[k], ref.at[:, 0, :], osem.at[k])

    for k, ref in ((2, direc), (0, sol), (1, res)):
        fetch(k, ref).start()
    step, ratio = scal[:, 0:1], scal[:, 1:2]
    fetch(2, direc).wait()
    put[2] = comb[...] + ratio * got[2]
    store(2, new_dir).start()
    fetch(0, sol).wait()
    put[0] = got[0] + step * got[2]
    store(0, new_sol).start()
    fetch(1, res).wait()
    put[1] = got[1] - step * image[...]
    store(1, new_res).start()
    for k, ref in ((2, new_dir), (0, new_sol), (1, new_res)):
        store(k, ref).wait()


def on_device(
    T, O, design, gap_flags, segment_ids, ar_order, ma_order, ar_roots, ma_roots,
    kaula, precond, solution, residual, direction,
):
    n = segment_ids.shape[0]
    columns = design.shape[2]
    share = direction.shape[2]
    rhs = direction.shape[0]
    blocks = precond.shape[1]
    f32, bf16 = jnp.float32, jnp.bfloat16
    A = T // 2
    vmem = pl.BlockSpec(memory_space=pltpu.VMEM)
    smem = pl.BlockSpec(memory_space=pltpu.SMEM)
    hbm = pl.BlockSpec(memory_space=pl.ANY)
    V, D = pltpu.VMEM, lambda k: pltpu.SemaphoreType.DMA((max(k, 1),))
    vec = jax.ShapeDtypeStruct((rhs, share), f32)
    image, comb, scal = pl.pallas_call(
        functools.partial(kernel, T, O),
        out_shape=[vec, vec, jax.ShapeDtypeStruct((rhs, 128), f32)],
        in_specs=[hbm, vmem, vmem, smem, smem, smem, smem, vmem, hbm, hbm, hbm],
        out_specs=[vmem] * 3,
        scratch_shapes=[
            V((T, 3 * n, share), bf16), V((blocks, 128, 128), f32), V((rhs, share), f32),
            V((rhs, share), f32), V((rhs, share), bf16), V((blocks, 128, 128), bf16),
            V((blocks, 128, 128), bf16),
            V((A, rhs, share), bf16), V((A, rhs, share), bf16),
            V((rhs, 3 * n), f32), V((O - 1, rhs, 3 * n), f32), V((T - 1, 1, n), jnp.int32),
            V((rhs // 2, n), f32), V((T - 1, rhs // 2, n), f32), V((3, n, n), f32),
            V((A, rhs, share), LINK), V((A, rhs, share), LINK),
            V((A, rhs, share), LINK), V((A, rhs, share), LINK),
            V((rhs, share), f32), V((rhs, share), f32),
            V((1, 128), f32), V((O - 1, 1, 128), f32), V((1, 128), f32), V((T - 1, 1, 128), f32),
            D(T), D(3), D(A), D(A), D(A), D(A), D(O - 1), D(O - 1),
            D(T - 1), D(T - 1), D(T - 1), D(T - 1), D(A), D(A), D(A),
            D(A), D(O - 1), D(O - 1), D(T - 1), D(T - 1),
        ],
        compiler_params=pltpu.CompilerParams(
            collective_id=0, has_side_effects=True, vmem_limit_bytes=56 * 1024 * 1024
        ),
    )(
        design.reshape(3 * n, columns), segment_ids.reshape(1, n), gap_flags.reshape(1, n),
        ar_roots, ma_roots, ar_order, ma_order, kaula, precond[0], residual, direction,
    )
    full = jax.ShapeDtypeStruct(direction.shape, f32)
    return tuple(
        pl.pallas_call(
            finish,
            out_shape=[full] * 3,
            in_specs=[vmem, vmem, vmem, hbm, hbm, hbm],
            out_specs=[hbm] * 3,
            scratch_shapes=[V((3, rhs, share), f32), V((3, rhs, share), f32), D(3), D(3)],
        )(image, comb, scal, solution, residual, direction)
    )


def solution(mesh):
    vec = P(None, "order", "tm")
    in_specs = (
        P(None, "tm", "order"), P("tm"), P("tm"), P(), P(), P(), P(), P("order", "tm"),
        P("order", "tm", None, None), vec, vec, vec,
    )
    body = functools.partial(on_device, mesh.shape["tm"], mesh.shape["order"])
    return jax.shard_map(
        body, mesh=mesh, in_specs=in_specs, out_specs=(vec, vec, vec), check_vma=False
    )
```

profile of v0, /device:TPU:0, one launch (start us, length us, event | category | flops | bytes accessed | tf_op | source)
XLA Modules:
  0.0 54.6 jit_solution(5538477261544252919)
XLA Ops:
  0.6 51.2 %shard_map.139 = (f32[16,2048]{1,0:T(8,128)}, f32[16,2048]{1,0:T(8,128)}, f32[16,128]{1,0:T(8,128)}) custom-call(bf16[384,16384]{1,0:T(8,128)(2,1)} %bitcast.4, s32[1,128]{1,0:T(1,128)} %bitcast.6, s32[1,128]{1,0:T(1,128)} %bitcast.7, f32[3,4]{1,0:T(4,128)} %ar_ref.1, f32[3,4]{1,0:T(4,128)} %ma_ref.1, s32[3]{0:T(128)} %aro_ref.1, s32[3]{0:T(128)} %mao_ref.1, ...), custom_call_target="tpu_custom_call" | custom-call | tf_op jit(solution)/shard_map/pallas_call | solution.py:430
  51.9 2.8 %shard_map.140 = (f32[16,1,2048]{2,1,0:T(1,128)}, f32[16,1,2048]{2,1,0:T(1,128)}, f32[16,1,2048]{2,1,0:T(1,128)}) custom-call(f32[16,2048]{1,0:T(8,128)} %get-tuple-element.6.image, f32[16,2048]{1,0:T(8,128)} %get-tuple-element.7.comb, f32[16,128]{1,0:T(8,128)} %get-tuple-element.8.scal, f32[16,1,2048]{2,1,0:T(1,128)} %sol.1, f32[16,1,2048]{2,1,0:T(1,128)} %res.1, ...), custom_call_target="tpu_custom_call" | custom-call | tf_op jit(solution)/shard_map/pallas_call | solution.py:459
where the time goes:
time: 54.9 us; the launch traced here: 54.6 us
  Pallas kernels  54 us (98%)
  between operations  0.64 us (1%)
    pallas_call x1, Pallas kernels, on_device(): pl.pallas_call(functools.partial(kernel, T, O), out_shape=[vec, vec, jax....  51.2 us
    pallas_call x1, Pallas kernels, on_device(): pl.pallas_call(finish, out_shape=[full] * 3, in_specs=[vmem, vmem, vmem,...  2.79 us

commit v1 on v0

v1 whole, which is shorter than its diff:
```python
import functools

import jax
import jax.numpy as jnp
from jax import lax
from jax.experimental import pallas as pl
from jax.experimental.pallas import tpu as pltpu
from jax.sharding import PartitionSpec as P

LINK = jnp.bfloat16
LAGS = 4
HI = lax.Precision.HIGHEST
NN = (((1,), (0,)), ((), ()))
NT = (((1,), (1,)), ((), ()))


def dot(a, b, dims, precision=None):
    return lax.dot_general(a, b, dims, precision=precision, preferred_element_type=jnp.float32)


def tall(block, rows):
    return jnp.concatenate(
        [block, jnp.zeros((rows - block.shape[0], block.shape[1]), jnp.float32)], axis=0
    )


def halves(x):
    top = x.astype(jnp.bfloat16)
    return top, (x - top.astype(jnp.float32)).astype(jnp.bfloat16)


def dot3(x, high, low, dims):
    rows = x.shape[0]
    top, rest = halves(x)
    both = dot(jnp.concatenate([top, rest], axis=0), high, dims)
    return both[:rows] + both[rows:] + dot(top, low, dims)


def bands(matrix):
    row = lax.broadcasted_iota(jnp.int32, matrix.shape, 0)
    col = lax.broadcasted_iota(jnp.int32, matrix.shape, 1)
    return [
        jnp.sum(jnp.where(row == col - 4 * shift, matrix, 0.0), axis=0, keepdims=True)
        for shift in range(1 - LAGS, LAGS)
    ]


def banded(vector, coeffs):
    width = vector.shape[1]
    total = None
    for shift, coeff in zip(range(1 - LAGS, LAGS), coeffs):
        moved = vector if shift == 0 else pltpu.roll(vector, 4 * shift % width, 1)
        total = moved * coeff if total is None else total + moved * coeff
    return total


def columns(ref, order_ref, comp):
    out = []
    for k in range(LAGS):
        column = jnp.zeros(comp.shape, jnp.float32)
        for c in range(3):
            value = jnp.where(k < order_ref[c], ref[c, k], 0.0)
            column = jnp.where(comp == c, value, column)
        out.append(column)
    return out


def stack(pieces):
    row = lax.broadcasted_iota(jnp.int32, pieces[0].shape, 0)
    real = row % 4 < 3
    both = [jnp.where(row < 4, pieces[i], pieces[i + 1]) for i in range(0, LAGS, 2)]
    return jnp.concatenate([jnp.where(real, block, 0.0) for block in both], axis=0)


def filters(ar_ref, ma_ref, aro_ref, mao_ref, ids, pt_ref):
    n = ids.shape[1]
    lane = lax.broadcasted_iota(jnp.int32, (8, n), 1)
    comp = lax.broadcasted_iota(jnp.int32, (8, n), 0) % 4

    def lagged(v, k):
        return v if k == 0 else jnp.where(lane >= k, pltpu.roll(v, k, 1), 0.0)

    def at(k):
        return jnp.where(lane == k, 1.0, 0.0)

    ar, ma = columns(ar_ref, aro_ref, comp), columns(ma_ref, mao_ref, comp)
    a, b = [1.0] + [0.0] * LAGS, [1.0] + [0.0] * LAGS
    for k in range(LAGS):
        a = [a[0]] + [a[j] - ar[k] * a[j - 1] for j in range(1, LAGS + 1)]
        b = [b[0]] + [b[j] - ma[k] * b[j - 1] for j in range(1, LAGS + 1)]
    h, power, m = at(0), ar, 1
    while m < n:
        s0, q0 = power[0] + power[1], power[0] * power[1]
        s1, q1 = power[2] + power[3], power[2] * power[3]
        e = [s0 + s1, q0 + q1 + s0 * s1, q0 * s1 + s0 * q1, q0 * q1]
        terms = [e[j] * lagged(h, (j + 1) * m) for j in range(LAGS) if (j + 1) * m < n]
        while len(terms) > 1:
            terms = [sum(terms[i + 1 : i + 2], terms[i]) for i in range(0, len(terms), 2)]
        h = h + terms[0]
        power, m = [p * p for p in power], 2 * m
    hs = [lagged(h, k) for k in range(LAGS + 1)]
    g = hs[0] + ((b[1] * hs[1] + b[2] * hs[2]) + (b[3] * hs[3] + b[4] * hs[4]))
    gs = [lagged(g, k) for k in range(LAGS)]
    ins, ends = [], []
    for i in range(1, LAGS + 1):
        acc, end = jnp.zeros_like(g), jnp.zeros_like(g)
        for k in range(LAGS + 1 - i):
            acc = acc + b[i + k] * at(k) - a[i + k] * gs[k]
            end = end - a[i + k] * at(n - 1 - k)
        ins.append(acc)
        ends.append(end)
    yield None
    row = lax.broadcasted_iota(jnp.int32, (n, n), 0)
    col = lax.broadcasted_iota(jnp.int32, (n, n), 1)
    grid = jnp.broadcast_to(ids, (n, n))
    joined = (grid == grid.T) & (col >= row)
    for c in range(3):
        t = pltpu.roll(jnp.broadcast_to(g[c : c + 1], (n, n)), 0, 1, stride=1, stride_axis=0)
        pt_ref[c] = jnp.where(joined, t, 0.0)
    yield None
    ca, ends = stack(hs[:LAGS]), stack(ends)
    flip = jnp.where(row + col == n - 1, 1.0, 0.0).astype(jnp.float32)
    ab = dot(stack(ins), flip, NN, HI)
    fwd = bands(dot(ca, tall(ends, n), NT, HI))
    bwd = bands(dot(ends, tall(ca, n), NT, HI))
    yield ca, ab, fwd, bwd


def spread(block, mask):
    row = lax.broadcasted_iota(jnp.int32, block.shape, 0)
    return jnp.concatenate(
        [jnp.where(row % 4 == c, block * mask, 0.0) for c in range(3)], axis=1
    )


def state_weights(T, me, shape, links, throughs, fwd, bwd, energies):
    row = lax.broadcasted_iota(jnp.int32, shape, 0)
    lane = lax.broadcasted_iota(jnp.int32, shape, 1)
    eye = jnp.where(row == lane, 1.0, 0.0)
    zero = jnp.zeros(shape, jnp.float32)
    state, ins, mine = {}, [], {}

    def keep(blocks, e, into):
        for key, v in blocks.items():
            mine[into, key] = jnp.where(me == e, v, mine.get((into, key), zero))

    for e in range(T):
        entering = {q: v * links[e] for q, v in state.items()}
        ins.append(entering)
        keep(entering, e, "in")
        state = {q: throughs[e] * banded(v, fwd) for q, v in entering.items()}
        state[e] = eye
    back = {}
    for e in range(T - 1, 0, -1):
        new = {key: throughs[e] * banded(v, bwd) for key, v in back.items()}
        for q, v in ins[e].items():
            moved = banded(v, energies[e])
            new["tail", q] = new["tail", q] + moved if ("tail", q) in new else moved
        new["head", e] = eye
        back = {key: v * links[e] for key, v in new.items()}
        keep(back, e - 1, "back")
    out = []
    for e in range(T):
        entering = pltpu.roll(mine["in", e], 16, 1) if ("in", e) in mine else zero
        out.append(mine.get(("back", ("tail", e)), zero) + entering)
        out.append(mine.get(("back", ("head", e)), zero))
    return jnp.concatenate(out, axis=0)


def kernel(
    T, O,
    design, ids_in, gaps_in, ar_ref, ma_ref, aro_ref, mao_ref, kaula, precond_in,
    res_in, direc_in,
    image_out, comb_out, scal_out,
    dv, precond, res, direc, packed, high, low,
    right_in, left_in, obs_out, obs_in, ids_all, part_out, part_in, summ_out, summ_in, pt,
    map_high, map_low, cross_high, cross_low,
    rs_right_out, rs_left_out, rs_right_in, rs_left_in, applied, image_applied,
    tot_out, tot_in,
    dsem, in_sem, agr_s, agr_r, agl_s, agl_r, ob_s, ob_r, id_s, id_r, pa_s, pa_r, su_s, su_r,
    rr_s, rr_r, rl_s, rl_r, t1_s, t1_r,
):
    me, order = lax.axis_index("tm"), lax.axis_index("order")
    A = T // 2
    rhs, share = packed.shape
    n = ids_in.shape[1]
    blocks = precond.shape[0]

    slow, fast = me // 2, me % 2
    partner = {"tm": 2 * slow + 1 - fast}

    def at_slow(k, other=0):
        row = 1 - fast if other else fast
        return 2 * lax.rem(slow + k + A, A) + row

    mesh_ids = pl.DeviceIdType.MESH

    def to_tm(k):
        return {"tm": lax.rem(me + k, T)}

    def to_order(k):
        return {"order": lax.rem(order + k, O)}

    def to_all(k, i):
        return {"tm": lax.rem(me + k, T), "order": lax.rem(order + i, O)}

    def load(k, other):
        q = at_slow(k, other)
        slot = other * A + k % A
        return pltpu.make_async_copy(
            design.at[:, pl.ds(pl.multiple_of(q * share, 128), share)],
            dv.at[slot],
            dsem.at[slot],
        )

    def remote(src, dst, ssem, rsem, to):
        return pltpu.make_async_remote_copy(
            src_ref=src, dst_ref=dst, send_sem=ssem, recv_sem=rsem,
            device_id=to, device_id_type=mesh_ids,
        )

    get_direc = pltpu.make_async_copy(direc_in.at[:, 0, :], direc, in_sem.at[0])
    get_res = pltpu.make_async_copy(res_in.at[:, 0, :], res, in_sem.at[1])
    get_precond = pltpu.make_async_copy(precond_in, precond, in_sem.at[2])
    get_direc.start()
    barrier = pltpu.get_barrier_semaphore()
    for k in range(1, T):
        pl.semaphore_signal(barrier, inc=1, device_id=to_tm(k), device_id_type=mesh_ids)
    for k in range(1, O):
        pl.semaphore_signal(barrier, inc=1, device_id=to_order(k), device_id_type=mesh_ids)
    for i in range(1, O):
        for k in range(1, T):
            pl.semaphore_signal(barrier, inc=1, device_id=to_all(k, i), device_id_type=mesh_ids)
    load(0, 0).start()
    get_precond.start()
    get_res.start()
    load(0, 1).start()
    for k in range(1, A):
        load(-k, 0).start()
        load(-k, 1).start()
    get_direc.wait()
    packed[...] = direc[...].astype(jnp.bfloat16)
    pl.semaphore_wait(barrier, T * O - 1)

    across = [remote(packed, right_in.at[k], agr_s.at[k], agr_r.at[k], {"tm": at_slow(k)})
              for k in range(1, A)]
    beside = [remote(packed, left_in.at[0], agl_s.at[0], agl_r.at[0], partner)]
    beside += [remote(right_in.at[k], left_in.at[k], agl_s.at[k], agl_r.at[k], partner)
               for k in range(1, A)]
    for copy in across + beside[:1]:
        copy.start()
    id_copies = [
        remote(ids_in, ids_all.at[k - 1], id_s.at[k - 1], id_r.at[k - 1], to_tm(k))
        for k in range(1, T)
    ]
    for copy in id_copies:
        copy.start()

    load(0, 0).wait()
    obs = dot(packed[...], dv[0], NT)
    ids = ids_in[0:1, :].astype(jnp.float32)
    gaps3 = jnp.concatenate([gaps_in[0:1, :].astype(jnp.float32)] * 3, axis=1)
    building = filters(ar_ref, ma_ref, aro_ref, mao_ref, ids, pt)
    next(building)

    def preconditioned(v, cols):
        out = []
        for m in range(cols.start // 128, cols.stop // 128):
            x = v[:, m * 128 - cols.start : (m + 1) * 128 - cols.start]
            out.append(dot3(x, high[m], low[m], NT))
        return jnp.concatenate(out, axis=1)

    def arrive(k):
        across[k - 1].wait_recv()
        beside[k].start()

    def right(k, obs):
        load(-k, 0).wait()
        return obs + dot(right_in[k], dv[(-k) % A], NT)

    def left(k, obs):
        beside[k].wait_recv()
        load(-k, 1).wait()
        return obs + dot(left_in[k], dv[A + (-k) % A], NT)

    arrive(1)
    next(building)
    ca, ab, fwd, bwd = next(building)
    first, last = ids[:, 0:1], ids[:, n - 1 : n]
    head_map = spread(ca, jnp.where(ids == first, 1.0, 0.0))
    tail_map = spread(ab, jnp.where(ids == last, 1.0, 0.0))
    head_map = jnp.concatenate(
        [dot(head_map[:, c * n : (c + 1) * n], pt[c], NT, HI) for c in range(3)], axis=1
    )
    both_maps = jnp.concatenate([tail_map, head_map], axis=0)
    slots = jnp.concatenate([both_maps] * (n // 32), axis=0)
    slot_row = lax.broadcasted_iota(jnp.int32, slots.shape, 0) // 32
    top, rest = halves(jnp.where(slot_row == lax.rem(me, n // 32), slots, 0.0))
    map_high[...] = top
    map_low[...] = rest
    obs = right(1, obs)
    obs = left(0, obs)
    get_precond.wait()
    for m in range(blocks):
        top, rest = halves(precond[m])
        high[m] = top
        low[m] = rest
    for k in range(2, A):
        arrive(k)
        obs = right(k, obs)
        obs = left(k - 1, obs)
    get_res.wait()
    applied[...] = preconditioned(res[...], slice(0, share))
    obs = left(A - 1, obs)

    half = rhs // 2
    summary = dot3(obs * gaps3, map_high[...], map_low[...], NT)
    part_out[...] = summary[:half] + pltpu.roll(summary[half:], n // 2, 1)
    obs_out[...] = obs
    pa_copies = [
        remote(part_out, part_in.at[k - 1], pa_s.at[k - 1], pa_r.at[k - 1], to_order(k))
        for k in range(1, O)
    ]
    ob_copies = [
        remote(obs_out, obs_in.at[k - 1], ob_s.at[k - 1], ob_r.at[k - 1], to_order(k))
        for k in range(1, O)
    ]
    for copy in pa_copies + ob_copies:
        copy.start()

    for copy in id_copies:
        copy.wait_recv()
    ids_e = []
    for e in range(T):
        slot = jnp.minimum(lax.rem(me - e + T - 1, T), T - 2)
        ids_e.append(jnp.where(me == e, ids, ids_all[slot].astype(jnp.float32)))
    firsts = [v[:, 0:1] for v in ids_e]
    lasts = [v[:, n - 1 : n] for v in ids_e]
    runs = jnp.concatenate(
        [ca * jnp.where(v == f, 1.0, 0.0) for v, f in zip(ids_e, firsts)], axis=0
    )
    energy = dot(runs, tall(ca, n), NT, HI)
    energies = [bands(energy[16 * e : 16 * e + 16]) for e in range(T)]
    links = [None] + [jnp.where(lasts[e - 1] == firsts[e], 1.0, 0.0) for e in range(1, T)]
    throughs = [jnp.where(firsts[e] == lasts[e], 1.0, 0.0) for e in range(T)]
    direct = T <= 8
    if direct:
        weights = state_weights(T, me, (16, n), links, throughs, fwd, bwd, energies)

    for copy in pa_copies:
        copy.wait_recv()
    summ_out[...] = part_out[...] + sum([part_in[k] for k in range(1, O - 1)], part_in[0])
    su_copies = [
        remote(summ_out, summ_in.at[k - 1], su_s.at[k - 1], su_r.at[k - 1], to_tm(k))
        for k in range(1, T)
    ]
    for copy in su_copies:
        copy.start()
    if direct:
        top, rest = halves(dot(weights, tall(both_maps, n), NN, HI))
        cross_high[...] = top
        cross_low[...] = rest
    for copy in ob_copies:
        copy.wait_recv()
    for k in range(1, O):
        obs = obs + obs_in[k - 1]
    masked = obs * gaps3
    local_back = jnp.concatenate(
        [
            dot(dot(masked[:, c * n : (c + 1) * n], pt[c], NN, HI), pt[c], NT, HI)
            for c in range(3)
        ],
        axis=1,
    )
    for copy in su_copies:
        copy.wait_recv()
    folded = []
    for e in range(T):
        slot = jnp.minimum(lax.rem(me - e + T - 1, T), T - 2)
        folded.append(jnp.where(me == e, summ_out[...], summ_in[slot]))
    lane8 = lax.broadcasted_iota(jnp.int32, (half, n), 1)
    groups = []
    for e in range(0, T, 4):
        front, back = folded[e] + folded[e + 1], folded[e + 2] + folded[e + 3]
        upper = jnp.where(lane8 < n // 2, front, back)
        lower = pltpu.roll(jnp.where(lane8 < n // 2, back, front), n // 2, 1)
        groups.append(jnp.concatenate([upper, lower], axis=0))
    if direct:
        adjoint = local_back + dot3(
            jnp.concatenate(groups, axis=1), cross_high[...], cross_low[...], NN
        )
    else:
        lane = lax.broadcasted_iota(jnp.int32, (rhs, n), 1)
        tails = [
            jnp.where(lane < 16, pltpu.roll(groups[e // 4], (n - 32 * (e % 4)) % n, 1), 0.0)
            for e in range(T)
        ]
        heads = [
            jnp.where(lane < 16, pltpu.roll(groups[e // 4], (n - 32 * (e % 4) - 16) % n, 1), 0.0)
            for e in range(T)
        ]
        state = jnp.zeros((rhs, n), jnp.float32)
        mine_in, mine_back, back, ins = state, state, state, []
        for e in range(T):
            entering = state if e == 0 else state * links[e]
            ins.append(entering)
            mine_in = jnp.where(me == e, entering, mine_in)
            state = tails[e] + throughs[e] * banded(entering, fwd)
        for e in range(T - 1, 0, -1):
            back = heads[e] + banded(ins[e], energies[e]) + throughs[e] * banded(back, bwd)
            back = back * links[e]
            mine_back = jnp.where(me == e - 1, back, mine_back)
        states = mine_back + pltpu.roll(mine_in, 16, 1)
        adjoint = local_back + dot(states, tall(both_maps, n), NN, HI)
    weighted = (adjoint * gaps3).astype(jnp.bfloat16)

    def grad(k, other):
        return dot(weighted, dv[other * A + k % A], NN)

    pair = [remote(rs_left_out.at[k], rs_left_in.at[k], rl_s.at[k], rl_r.at[k], partner)
            for k in range(A)]
    far = [remote(rs_right_out.at[k], rs_right_in.at[k], rr_s.at[k], rr_r.at[k],
                  {"tm": at_slow(k)}) for k in range(1, A)]
    order_of = list(range(1, A)) + [0]
    for k in order_of:
        rs_left_out[k] = grad(k, 1).astype(LINK)
        pair[k].start()
    for k in order_of[:-1]:
        piece = grad(k, 0)
        pair[k].wait_recv()
        rs_right_out[k] = (piece + rs_left_in[k].astype(jnp.float32)).astype(LINK)
        far[k - 1].start()
    image = grad(0, 0) + kaula[...] * direc[...]
    pair[0].wait_recv()
    image = image + rs_left_in[0].astype(jnp.float32)
    for k in order_of[:-1]:
        far[k - 1].wait_recv()
        image = image + rs_right_in[k].astype(jnp.float32)
    image_applied[...] = preconditioned(image, slice(0, share))
    image_out[...] = image
    app, imapp = applied[...], image_applied[...]
    d, r = direc[...], res[...]
    lane = lax.broadcasted_iota(jnp.int32, (rhs, 128), 1)
    row = lax.broadcasted_iota(jnp.int32, (rhs, 128), 0)
    products = [r * app, d * image, image * app, image * imapp]
    total = jnp.zeros((rhs, 128), jnp.float32)
    for q, product in enumerate(products):
        total = jnp.where(lane == q * rhs + row, jnp.sum(product, axis=1, keepdims=True), total)
    total = jnp.sum(total, axis=0, keepdims=True)

    tot_out[...] = total
    tot_copies = []
    for i in range(O):
        for k in range(T):
            if i or k:
                at = i * T + k - 1
                tot_copies.append(
                    remote(tot_out, tot_in.at[at], t1_s.at[at], t1_r.at[at], to_all(k, i))
                )
    for copy in tot_copies:
        copy.start()
    for copy in tot_copies:
        copy.wait_recv()
    total = total + jnp.sum(tot_in[...], axis=0)
    wide = jnp.broadcast_to(total[0:1, :], (rhs, 128))
    old_rz, curvature, cross, quad = [
        jnp.sum(jnp.where(lane == q * rhs + row, wide, 0.0), axis=1, keepdims=True)
        for q in range(4)
    ]
    step = old_rz / curvature
    new_rz = old_rz - 2.0 * step * cross + step * step * quad
    comb_out[...] = app - step * imapp
    scal_out[...] = jnp.where(lane == 0, step, new_rz / old_rz)

    for copy in across + beside + pair + far:
        copy.wait_send()
    for copy in id_copies + pa_copies + ob_copies + su_copies + tot_copies:
        copy.wait_send()


def finish(image, comb, scal, sol, res, direc, new_sol, new_res, new_dir, got, put, isem, osem):
    def fetch(k, ref):
        return pltpu.make_async_copy(ref.at[:, 0, :], got.at[k], isem.at[k])

    def store(k, ref):
        return pltpu.make_async_copy(put.at[k], ref.at[:, 0, :], osem.at[k])

    for k, ref in ((2, direc), (0, sol), (1, res)):
        fetch(k, ref).start()
    step, ratio = scal[:, 0:1], scal[:, 1:2]
    fetch(2, direc).wait()
    put[2] = comb[...] + ratio * got[2]
    store(2, new_dir).start()
    fetch(0, sol).wait()
    put[0] = got[0] + step * got[2]
    store(0, new_sol).start()
    fetch(1, res).wait()
    put[1] = got[1] - step * image[...]
    store(1, new_res).start()
    for k, ref in ((2, new_dir), (0, new_sol), (1, new_res)):
        store(k, ref).wait()


def on_device(
    T, O, design, gap_flags, segment_ids, ar_order, ma_order, ar_roots, ma_roots,
    kaula, precond, solution, residual, direction,
):
    n = segment_ids.shape[0]
    columns = design.shape[2]
    share = direction.shape[2]
    rhs = direction.shape[0]
    blocks = precond.shape[1]
    f32, bf16 = jnp.float32, jnp.bfloat16
    A = T // 2
    vmem = pl.BlockSpec(memory_space=pltpu.VMEM)
    smem = pl.BlockSpec(memory_space=pltpu.SMEM)
    hbm = pl.BlockSpec(memory_space=pl.ANY)
    V, D = pltpu.VMEM, lambda k: pltpu.SemaphoreType.DMA((max(k, 1),))
    vec = jax.ShapeDtypeStruct((rhs, share), f32)
    image, comb, scal = pl.pallas_call(
        functools.partial(kernel, T, O),
        out_shape=[vec, vec, jax.ShapeDtypeStruct((rhs, 128), f32)],
        in_specs=[hbm, vmem, vmem, smem, smem, smem, smem, vmem, hbm, hbm, hbm],
        out_specs=[vmem] * 3,
        scratch_shapes=[
            V((T, 3 * n, share), bf16), V((blocks, 128, 128), f32), V((rhs, share), f32),
            V((rhs, share), f32), V((rhs, share), bf16), V((blocks, 128, 128), bf16),
            V((blocks, 128, 128), bf16),
            V((A, rhs, share), bf16), V((A, rhs, share), bf16),
            V((rhs, 3 * n), f32), V((O - 1, rhs, 3 * n), f32), V((T - 1, 1, n), jnp.int32),
            V((rhs // 2, n), f32), V((O - 1, rhs // 2, n), f32),
            V((rhs // 2, n), f32), V((T - 1, rhs // 2, n), f32), V((3, n, n), f32),
            V((n, 3 * n), bf16), V((n, 3 * n), bf16), V((32 * T, 3 * n), bf16), V((32 * T, 3 * n), bf16),
            V((A, rhs, share), LINK), V((A, rhs, share), LINK),
            V((A, rhs, share), LINK), V((A, rhs, share), LINK),
            V((rhs, share), f32), V((rhs, share), f32),
            V((1, 128), f32), V((T * O - 1, 1, 128), f32),
            D(T), D(3), D(A), D(A), D(A), D(A), D(O - 1), D(O - 1),
            D(T - 1), D(T - 1), D(O - 1), D(O - 1), D(T - 1), D(T - 1), D(A), D(A), D(A),
            D(A), D(T * O - 1), D(T * O - 1),
        ],
        compiler_params=pltpu.CompilerParams(
            collective_id=0, has_side_effects=True, vmem_limit_bytes=56 * 1024 * 1024
        ),
    )(
        design.reshape(3 * n, columns), segment_ids.reshape(1, n), gap_flags.reshape(1, n),
        ar_roots, ma_roots, ar_order, ma_order, kaula, precond[0], residual, direction,
    )
    full = jax.ShapeDtypeStruct(direction.shape, f32)
    return tuple(
        pl.pallas_call(
            finish,
            out_shape=[full] * 3,
            in_specs=[vmem, vmem, vmem, hbm, hbm, hbm],
            out_specs=[hbm] * 3,
            scratch_shapes=[V((3, rhs, share), f32), V((3, rhs, share), f32), D(3), D(3)],
        )(image, comb, scal, solution, residual, direction)
    )


def solution(mesh):
    vec = P(None, "order", "tm")
    in_specs = (
        P(None, "tm", "order"), P("tm"), P("tm"), P(), P(), P(), P(), P("order", "tm"),
        P("order", "tm", None, None), vec, vec, vec,
    )
    body = functools.partial(on_device, mesh.shape["tm"], mesh.shape["order"])
    return jax.shard_map(
        body, mesh=mesh, in_specs=in_specs, out_specs=(vec, vec, vec), check_vma=False
    )
```

time: 54.9 us -> 50.8 us (0.925)
  Pallas kernels: 54 us -> 49.9 us
    pallas_call x1, Pallas kernels: 51.2 us -> 47.1 us  [on_device(): pl.pallas_call(functools.partial(kernel, T, O), out_shape=[vec, vec, jax....]
where the time goes in v1:
time: 50.8 us; the launch traced here: 50.6 us
  Pallas kernels  49.9 us (98%)
  between operations  0.64 us (1%)
    pallas_call x1, Pallas kernels, on_device(): pl.pallas_call(functools.partial(kernel, T, O), out_shape=[vec, vec, jax....  47.1 us
    pallas_call x1, Pallas kernels, on_device(): pl.pallas_call(finish, out_shape=[full] * 3, in_specs=[vmem, vmem, vmem,...  2.79 us

profile of v1, /device:TPU:0, one launch (start us, length us, event | category | flops | bytes accessed | tf_op | source)
XLA Modules:
  0.0 50.6 jit_solution(16125126504634781199)
XLA Ops:
  0.6 47.1 %shard_map.139 = (f32[16,2048]{1,0:T(8,128)}, f32[16,2048]{1,0:T(8,128)}, f32[16,128]{1,0:T(8,128)}) custom-call(bf16[384,16384]{1,0:T(8,128)(2,1)} %bitcast.4, s32[1,128]{1,0:T(1,128)} %bitcast.6, s32[1,128]{1,0:T(1,128)} %bitcast.7, f32[3,4]{1,0:T(4,128)} %ar_ref.1, f32[3,4]{1,0:T(4,128)} %ma_ref.1, s32[3]{0:T(128)} %aro_ref.1, s32[3]{0:T(128)} %mao_ref.1, ...), custom_call_target="tpu_custom_call" | custom-call | tf_op jit(solution)/shard_map/pallas_call | solution.py:520
  47.8 2.8 %shard_map.140 = (f32[16,1,2048]{2,1,0:T(1,128)}, f32[16,1,2048]{2,1,0:T(1,128)}, f32[16,1,2048]{2,1,0:T(1,128)}) custom-call(f32[16,2048]{1,0:T(8,128)} %get-tuple-element.6.image, f32[16,2048]{1,0:T(8,128)} %get-tuple-element.7.comb, f32[16,128]{1,0:T(8,128)} %get-tuple-element.8.scal, f32[16,1,2048]{2,1,0:T(1,128)} %sol.1, f32[16,1,2048]{2,1,0:T(1,128)} %res.1, ...), custom_call_target="tpu_custom_call" | custom-call | tf_op jit(solution)/shard_map/pallas_call | solution.py:551

commit v2 on v1

--- a/solution.py
+++ b/solution.py
@@ -9,6 +9,7 @@
 
 LINK = jnp.bfloat16
 LAGS = 4
+CHUNKS = 2
 HI = lax.Precision.HIGHEST
 NN = (((1,), (0,)), ((), ()))
 NT = (((1,), (1,)), ((), ()))
@@ -172,26 +173,32 @@
     design, ids_in, gaps_in, ar_ref, ma_ref, aro_ref, mao_ref, kaula, precond_in,
     res_in, direc_in,
     image_out, comb_out, scal_out,
-    dv, precond, res, direc, packed, high, low,
-    right_in, left_in, obs_out, obs_in, ids_all, part_out, part_in, summ_out, summ_in, pt,
-    map_high, map_low, cross_high, cross_low,
-    rs_right_out, rs_left_out, rs_right_in, rs_left_in, applied, image_applied,
+    dv, precond, res, direc, packed, high, low_part,
+    got, obs_out, obs_in, ids_all, part_out, part_in, summ_out, summ_in, pt,
+    map_high, map_low, cross_high, cross_low, rs_out, rs_in, applied, image_applied,
     tot_out, tot_in,
-    dsem, in_sem, agr_s, agr_r, agl_s, agl_r, ob_s, ob_r, id_s, id_r, pa_s, pa_r, su_s, su_r,
-    rr_s, rr_r, rl_s, rl_r, t1_s, t1_r,
+    dsem, in_sem, ga_s, ga_r, ob_s, ob_r, id_s, id_r, pa_s, pa_r, su_s, su_r,
+    rs_s, rs_r, t1_s, t1_r,
 ):
     me, order = lax.axis_index("tm"), lax.axis_index("order")
-    A = T // 2
     rhs, share = packed.shape
     n = ids_in.shape[1]
     blocks = precond.shape[0]
-
-    slow, fast = me // 2, me % 2
-    partner = {"tm": 2 * slow + 1 - fast}
-
-    def at_slow(k, other=0):
-        row = 1 - fast if other else fast
-        return 2 * lax.rem(slow + k + A, A) + row
+    wide = share // CHUNKS
+    bits = T.bit_length() - 1
+
+    def low(x):
+        return (x & -x).bit_length() - 1 if x else bits
+
+    def across(x):
+        out = me
+        for b in range(bits):
+            if x >> b & 1:
+                out = out + (1 << b) * (1 - 2 * lax.rem(lax.div(me, 1 << b), 2))
+        return out
+
+    def cols(c):
+        return slice(c * wide, (c + 1) * wide)
 
     mesh_ids = pl.DeviceIdType.MESH
 
@@ -204,13 +211,11 @@
     def to_all(k, i):
         return {"tm": lax.rem(me + k, T), "order": lax.rem(order + i, O)}
 
-    def load(k, other):
-        q = at_slow(k, other)
-        slot = other * A + k % A
+    def load(x):
         return pltpu.make_async_copy(
-            design.at[:, pl.ds(pl.multiple_of(q * share, 128), share)],
-            dv.at[slot],
-            dsem.at[slot],
+            design.at[:, pl.ds(pl.multiple_of(across(x) * share, 128), share)],
+            dv.at[x],
+            dsem.at[x],
         )
 
     def remote(src, dst, ssem, rsem, to):
@@ -224,66 +229,67 @@
     get_precond = pltpu.make_async_copy(precond_in, precond, in_sem.at[2])
     get_direc.start()
     barrier = pltpu.get_barrier_semaphore()
-    for k in range(1, T):
-        pl.semaphore_signal(barrier, inc=1, device_id=to_tm(k), device_id_type=mesh_ids)
+    for b in range(bits):
+        pl.semaphore_signal(
+            barrier, inc=1, device_id={"tm": across(1 << b)}, device_id_type=mesh_ids
+        )
     for k in range(1, O):
         pl.semaphore_signal(barrier, inc=1, device_id=to_order(k), device_id_type=mesh_ids)
-    for i in range(1, O):
-        for k in range(1, T):
-            pl.semaphore_signal(barrier, inc=1, device_id=to_all(k, i), device_id_type=mesh_ids)
-    load(0, 0).start()
+    plan = [4, 2, 1, 6, 3, 5, 7] if T == 8 else sorted(range(1, T), key=lambda x: -low(x))
+    load(0).start()
+    for x in plan:
+        load(x).start()
     get_precond.start()
     get_res.start()
-    load(0, 1).start()
-    for k in range(1, A):
-        load(-k, 0).start()
-        load(-k, 1).start()
     get_direc.wait()
     packed[...] = direc[...].astype(jnp.bfloat16)
-    pl.semaphore_wait(barrier, T * O - 1)
-
-    across = [remote(packed, right_in.at[k], agr_s.at[k], agr_r.at[k], {"tm": at_slow(k)})
-              for k in range(1, A)]
-    beside = [remote(packed, left_in.at[0], agl_s.at[0], agl_r.at[0], partner)]
-    beside += [remote(right_in.at[k], left_in.at[k], agl_s.at[k], agl_r.at[k], partner)
-               for k in range(1, A)]
-    for copy in across + beside[:1]:
-        copy.start()
-    id_copies = [
-        remote(ids_in, ids_all.at[k - 1], id_s.at[k - 1], id_r.at[k - 1], to_tm(k))
-        for k in range(1, T)
-    ]
-    for copy in id_copies:
-        copy.start()
-
-    load(0, 0).wait()
+    pl.semaphore_wait(barrier, bits + O - 1)
+
+    id_copies, ga_copies = {}, {}
+
+    def pass_on(x, c):
+        for b in reversed(range(low(x))):
+            to = x | 1 << b
+            if c == 0:
+                id_copies[to] = remote(
+                    ids_all.at[x - 1] if x else ids_in, ids_all.at[to - 1],
+                    id_s.at[to - 1], id_r.at[to - 1], {"tm": across(1 << b)},
+                )
+                id_copies[to].start()
+            ga_copies[to, c] = remote(
+                (got.at[x - 1] if x else packed).at[:, cols(c)], got.at[to - 1, :, cols(c)],
+                ga_s.at[to - 1, c], ga_r.at[to - 1, c], {"tm": across(1 << b)},
+            )
+            ga_copies[to, c].start()
+
+    def arrive(x, c):
+        if c == 0:
+            id_copies[x].wait_recv()
+        ga_copies[x, c].wait_recv()
+        pass_on(x, c)
+
+    for c in range(CHUNKS):
+        pass_on(0, c)
+
+    load(0).wait()
     obs = dot(packed[...], dv[0], NT)
     ids = ids_in[0:1, :].astype(jnp.float32)
     gaps3 = jnp.concatenate([gaps_in[0:1, :].astype(jnp.float32)] * 3, axis=1)
     building = filters(ar_ref, ma_ref, aro_ref, mao_ref, ids, pt)
     next(building)
 
-    def preconditioned(v, cols):
+    def preconditioned(v, at):
         out = []
-        for m in range(cols.start // 128, cols.stop // 128):
-            x = v[:, m * 128 - cols.start : (m + 1) * 128 - cols.start]
-            out.append(dot3(x, high[m], low[m], NT))
+        for m in range(at.start // 128, at.stop // 128):
+            x = v[:, m * 128 - at.start : (m + 1) * 128 - at.start]
+            out.append(dot3(x, high[m], low_part[m], NT))
         return jnp.concatenate(out, axis=1)
 
-    def arrive(k):
-        across[k - 1].wait_recv()
-        beside[k].start()
-
-    def right(k, obs):
-        load(-k, 0).wait()
-        return obs + dot(right_in[k], dv[(-k) % A], NT)
-
-    def left(k, obs):
-        beside[k].wait_recv()
-        load(-k, 1).wait()
-        return obs + dot(left_in[k], dv[A + (-k) % A], NT)
-
-    arrive(1)
+    def observe(x, c, obs):
+        if c == 0:
+            load(x).wait()
+        return obs + dot(got[x - 1, :, cols(c)], dv[x, :, cols(c)], NT)
+
     next(building)
     ca, ab, fwd, bwd = next(building)
     first, last = ids[:, 0:1], ids[:, n - 1 : n]
@@ -298,21 +304,16 @@
     top, rest = halves(jnp.where(slot_row == lax.rem(me, n // 32), slots, 0.0))
     map_high[...] = top
     map_low[...] = rest
-    obs = right(1, obs)
-    obs = left(0, obs)
-    get_precond.wait()
-    for m in range(blocks):
-        top, rest = halves(precond[m])
-        high[m] = top
-        low[m] = rest
-    for k in range(2, A):
-        arrive(k)
-        obs = right(k, obs)
-        obs = left(k - 1, obs)
-    get_res.wait()
-    applied[...] = preconditioned(res[...], slice(0, share))
-    obs = left(A - 1, obs)
-
+    steps = [("a", 4), ("a", 2), ("a", 1), ("o", 1), ("o", 4), ("a", 6), ("o", 2), ("o", 6),
+             ("b", 3), ("b", 5), ("b", 7)]
+    if T != 8:
+        steps = [("b", x) for x in plan]
+    for what, x in steps:
+        for c in range(CHUNKS):
+            if what != "o":
+                arrive(x, c)
+            if what != "a":
+                obs = observe(x, c, obs)
     half = rhs // 2
     summary = dot3(obs * gaps3, map_high[...], map_low[...], NT)
     part_out[...] = summary[:half] + pltpu.roll(summary[half:], n // 2, 1)
@@ -328,12 +329,12 @@
     for copy in pa_copies + ob_copies:
         copy.start()
 
-    for copy in id_copies:
-        copy.wait_recv()
     ids_e = []
     for e in range(T):
-        slot = jnp.minimum(lax.rem(me - e + T - 1, T), T - 2)
-        ids_e.append(jnp.where(me == e, ids, ids_all[slot].astype(jnp.float32)))
+        v = ids
+        for x in range(1, T):
+            v = jnp.where(across(x) == e, ids_all[x - 1].astype(jnp.float32), v)
+        ids_e.append(v)
     firsts = [v[:, 0:1] for v in ids_e]
     lasts = [v[:, n - 1 : n] for v in ids_e]
     runs = jnp.concatenate(
@@ -372,6 +373,13 @@
         ],
         axis=1,
     )
+    get_precond.wait()
+    for m in range(blocks):
+        top, rest = halves(precond[m])
+        high[m] = top
+        low_part[m] = rest
+    get_res.wait()
+    applied[...] = preconditioned(res[...], slice(0, share))
     for copy in su_copies:
         copy.wait_recv()
     folded = []
@@ -414,30 +422,30 @@
         adjoint = local_back + dot(states, tall(both_maps, n), NN, HI)
     weighted = (adjoint * gaps3).astype(jnp.bfloat16)
 
-    def grad(k, other):
-        return dot(weighted, dv[other * A + k % A], NN)
-
-    pair = [remote(rs_left_out.at[k], rs_left_in.at[k], rl_s.at[k], rl_r.at[k], partner)
-            for k in range(A)]
-    far = [remote(rs_right_out.at[k], rs_right_in.at[k], rr_s.at[k], rr_r.at[k],
-                  {"tm": at_slow(k)}) for k in range(1, A)]
-    order_of = list(range(1, A)) + [0]
-    for k in order_of:
-        rs_left_out[k] = grad(k, 1).astype(LINK)
-        pair[k].start()
-    for k in order_of[:-1]:
-        piece = grad(k, 0)
-        pair[k].wait_recv()
-        rs_right_out[k] = (piece + rs_left_in[k].astype(jnp.float32)).astype(LINK)
-        far[k - 1].start()
-    image = grad(0, 0) + kaula[...] * direc[...]
-    pair[0].wait_recv()
-    image = image + rs_left_in[0].astype(jnp.float32)
-    for k in order_of[:-1]:
-        far[k - 1].wait_recv()
-        image = image + rs_right_in[k].astype(jnp.float32)
-    image_applied[...] = preconditioned(image, slice(0, share))
-    image_out[...] = image
+    rs_copies = {}
+
+    def sum_of(x, c):
+        total = dot(weighted, dv[x, :, cols(c)], NN)
+        if x == 0:
+            total = total + kaula[:, cols(c)] * direc[:, cols(c)]
+        for b in range(low(x)):
+            rs_copies[x | 1 << b, c].wait_recv()
+            total = total + rs_in[(x | 1 << b) - 1, :, cols(c)].astype(jnp.float32)
+        return total
+
+    for x in [7, 5, 3, 1, 6, 4, 2] if T == 8 else sorted(range(1, T), key=lambda x: (low(x), -x)):
+        for c in range(CHUNKS):
+            rs_out[x - 1, :, cols(c)] = sum_of(x, c).astype(LINK)
+            rs_copies[x, c] = remote(
+                rs_out.at[x - 1, :, cols(c)], rs_in.at[x - 1, :, cols(c)],
+                rs_s.at[x - 1, c], rs_r.at[x - 1, c], {"tm": across(1 << low(x))},
+            )
+            rs_copies[x, c].start()
+    for c in range(CHUNKS):
+        piece = sum_of(0, c)
+        image_out[:, cols(c)] = piece
+        image_applied[:, cols(c)] = preconditioned(piece, cols(c))
+    image = image_out[...]
     app, imapp = applied[...], image_applied[...]
     d, r = direc[...], res[...]
     lane = lax.broadcasted_iota(jnp.int32, (rhs, 128), 1)
@@ -472,9 +480,10 @@
     comb_out[...] = app - step * imapp
     scal_out[...] = jnp.where(lane == 0, step, new_rz / old_rz)
 
-    for copy in across + beside + pair + far:
-        copy.wait_send()
-    for copy in id_copies + pa_copies + ob_copies + su_copies + tot_copies:
+    for copies in (id_copies, ga_copies, rs_copies):
+        for copy in copies.values():
+            copy.wait_send()
+    for copy in pa_copies + ob_copies + su_copies + tot_copies:
         copy.wait_send()
 
 
@@ -511,11 +520,10 @@
     rhs = direction.shape[0]
     blocks = precond.shape[1]
     f32, bf16 = jnp.float32, jnp.bfloat16
-    A = T // 2
     vmem = pl.BlockSpec(memory_space=pltpu.VMEM)
     smem = pl.BlockSpec(memory_space=pltpu.SMEM)
     hbm = pl.BlockSpec(memory_space=pl.ANY)
-    V, D = pltpu.VMEM, lambda k: pltpu.SemaphoreType.DMA((max(k, 1),))
+    V, D = pltpu.VMEM, lambda *k: pltpu.SemaphoreType.DMA(k)
     vec = jax.ShapeDtypeStruct((rhs, share), f32)
     image, comb, scal = pl.pallas_call(
         functools.partial(kernel, T, O),
@@ -526,18 +534,17 @@
             V((T, 3 * n, share), bf16), V((blocks, 128, 128), f32), V((rhs, share), f32),
             V((rhs, share), f32), V((rhs, share), bf16), V((blocks, 128, 128), bf16),
             V((blocks, 128, 128), bf16),
-            V((A, rhs, share), bf16), V((A, rhs, share), bf16),
+            V((T - 1, rhs, share), bf16),
             V((rhs, 3 * n), f32), V((O - 1, rhs, 3 * n), f32), V((T - 1, 1, n), jnp.int32),
             V((rhs // 2, n), f32), V((O - 1, rhs // 2, n), f32),
             V((rhs // 2, n), f32), V((T - 1, rhs // 2, n), f32), V((3, n, n), f32),
             V((n, 3 * n), bf16), V((n, 3 * n), bf16), V((32 * T, 3 * n), bf16), V((32 * T, 3 * n), bf16),
-            V((A, rhs, share), LINK), V((A, rhs, share), LINK),
-            V((A, rhs, share), LINK), V((A, rhs, share), LINK),
+            V((T - 1, rhs, share), LINK), V((T - 1, rhs, share), LINK),
             V((rhs, share), f32), V((rhs, share), f32),
             V((1, 128), f32), V((T * O - 1, 1, 128), f32),
-            D(T), D(3), D(A), D(A), D(A), D(A), D(O - 1), D(O - 1),
-            D(T - 1), D(T - 1), D(O - 1), D(O - 1), D(T - 1), D(T - 1), D(A), D(A), D(A),
-            D(A), D(T * O - 1), D(T * O - 1),
+            D(T), D(3), D(T - 1, CHUNKS), D(T - 1, CHUNKS), D(O - 1), D(O - 1),
+            D(T - 1), D(T - 1), D(O - 1), D(O - 1), D(T - 1), D(T - 1),
+            D(T - 1, CHUNKS), D(T - 1, CHUNKS), D(T * O - 1), D(T * O - 1),
         ],
         compiler_params=pltpu.CompilerParams(
             collective_id=0, has_side_effects=True, vmem_limit_bytes=56 * 1024 * 1024

time: 50.8 us -> 46.8 us (0.921)
  Pallas kernels: 49.9 us -> 45.9 us
    pallas_call x1, Pallas kernels: 47.1 us -> 43.1 us  [on_device(): pl.pallas_call(functools.partial(kernel, T, O), out_shape=[vec, vec, jax....]
where the time goes in v2:
time: 46.8 us; the launch traced here: 46.6 us
  Pallas kernels  45.9 us (98%)
  between operations  0.64 us (1%)
    pallas_call x1, Pallas kernels, on_device(): pl.pallas_call(functools.partial(kernel, T, O), out_shape=[vec, vec, jax....  43.1 us
    pallas_call x1, Pallas kernels, on_device(): pl.pallas_call(finish, out_shape=[full] * 3, in_specs=[vmem, vmem, vmem,...  2.79 us

profile of v2, /device:TPU:0, one launch (start us, length us, event | category | flops | bytes accessed | tf_op | source)
XLA Modules:
  0.0 46.6 jit_solution(17431384479646754380)
XLA Ops:
  0.6 43.1 %shard_map.139 = (f32[16,2048]{1,0:T(8,128)}, f32[16,2048]{1,0:T(8,128)}, f32[16,128]{1,0:T(8,128)}) custom-call(bf16[384,16384]{1,0:T(8,128)(2,1)} %bitcast.4, s32[1,128]{1,0:T(1,128)} %bitcast.6, s32[1,128]{1,0:T(1,128)} %bitcast.7, f32[3,4]{1,0:T(4,128)} %ar_ref.1, f32[3,4]{1,0:T(4,128)} %ma_ref.1, s32[3]{0:T(128)} %aro_ref.1, s32[3]{0:T(128)} %mao_ref.1, ...), custom_call_target="tpu_custom_call" | custom-call | tf_op jit(solution)/shard_map/pallas_call | solution.py:528
  43.8 2.8 %shard_map.140 = (f32[16,1,2048]{2,1,0:T(1,128)}, f32[16,1,2048]{2,1,0:T(1,128)}, f32[16,1,2048]{2,1,0:T(1,128)}) custom-call(f32[16,2048]{1,0:T(8,128)} %get-tuple-element.6.image, f32[16,2048]{1,0:T(8,128)} %get-tuple-element.7.comb, f32[16,128]{1,0:T(8,128)} %get-tuple-element.8.scal, f32[16,1,2048]{2,1,0:T(1,128)} %sol.1, f32[16,1,2048]{2,1,0:T(1,128)} %res.1, ...), custom_call_target="tpu_custom_call" | custom-call | tf_op jit(solution)/shard_map/pallas_call | solution.py:558

commit v3 on v2

--- a/solution.py
+++ b/solution.py
@@ -170,11 +170,11 @@
 
 def kernel(
     T, O,
-    design, ids_in, gaps_in, ar_ref, ma_ref, aro_ref, mao_ref, kaula, precond_in,
-    res_in, direc_in,
-    image_out, comb_out, scal_out,
-    dv, precond, res, direc, packed, high, low_part,
-    got, obs_out, obs_in, ids_all, part_out, part_in, summ_out, summ_in, pt,
+    design, ids_hbm, gaps_hbm, ar_hbm, ma_hbm, aro_hbm, mao_hbm, kaula_hbm, precond_in,
+    sol_in, res_in, direc_in,
+    new_sol, new_res, new_dir,
+    ids_in, gaps_in, ar_ref, ma_ref, aro_ref, mao_ref, kaula, dv, precond, sol, res, direc, packed, high, low_part,
+    image_out, got, obs_out, obs_in, ids_all, part_out, part_in, summ_out, summ_in, pt,
     map_high, map_low, cross_high, cross_low, rs_out, rs_in, applied, image_applied,
     tot_out, tot_in,
     dsem, in_sem, ga_s, ga_r, ob_s, ob_r, id_s, id_r, pa_s, pa_r, su_s, su_r,
@@ -226,8 +226,16 @@
 
     get_direc = pltpu.make_async_copy(direc_in.at[:, 0, :], direc, in_sem.at[0])
     get_res = pltpu.make_async_copy(res_in.at[:, 0, :], res, in_sem.at[1])
+    get_sol = pltpu.make_async_copy(sol_in.at[:, 0, :], sol, in_sem.at[3])
     get_precond = pltpu.make_async_copy(precond_in, precond, in_sem.at[2])
     get_direc.start()
+    get_small = [
+        pltpu.make_async_copy(src, dst, in_sem.at[4 + k])
+        for k, (src, dst) in enumerate((
+            (ids_hbm, ids_in), (ar_hbm, ar_ref), (ma_hbm, ma_ref), (aro_hbm, aro_ref),
+            (mao_hbm, mao_ref), (gaps_hbm, gaps_in), (kaula_hbm, kaula),
+        ))
+    ]
     barrier = pltpu.get_barrier_semaphore()
     for b in range(bits):
         pl.semaphore_signal(
@@ -236,13 +244,17 @@
     for k in range(1, O):
         pl.semaphore_signal(barrier, inc=1, device_id=to_order(k), device_id_type=mesh_ids)
     plan = [4, 2, 1, 6, 3, 5, 7] if T == 8 else sorted(range(1, T), key=lambda x: -low(x))
+    for copy in get_small:
+        copy.start()
     load(0).start()
     for x in plan:
         load(x).start()
     get_precond.start()
     get_res.start()
+    get_sol.start()
     get_direc.wait()
     packed[...] = direc[...].astype(jnp.bfloat16)
+    get_small[0].wait()
     pl.semaphore_wait(barrier, bits + O - 1)
 
     id_copies, ga_copies = {}, {}
@@ -271,6 +283,8 @@
     for c in range(CHUNKS):
         pass_on(0, c)
 
+    for copy in get_small[1:]:
+        copy.wait()
     load(0).wait()
     obs = dot(packed[...], dv[0], NT)
     ids = ids_in[0:1, :].astype(jnp.float32)
@@ -446,6 +460,7 @@
         image_out[:, cols(c)] = piece
         image_applied[:, cols(c)] = preconditioned(piece, cols(c))
     image = image_out[...]
+    get_sol.wait()
     app, imapp = applied[...], image_applied[...]
     d, r = direc[...], res[...]
     lane = lax.broadcasted_iota(jnp.int32, (rhs, 128), 1)
@@ -477,9 +492,9 @@
     ]
     step = old_rz / curvature
     new_rz = old_rz - 2.0 * step * cross + step * step * quad
-    comb_out[...] = app - step * imapp
-    scal_out[...] = jnp.where(lane == 0, step, new_rz / old_rz)
-
+    new_sol[...] = sol[...] + step * d
+    new_res[...] = r - step * image
+    new_dir[...] = app - step * imapp + (new_rz / old_rz) * d
     for copies in (id_copies, ga_copies, rs_copies):
         for copy in copies.values():
             copy.wait_send()
@@ -487,27 +502,17 @@
         copy.wait_send()
 
 
-def finish(image, comb, scal, sol, res, direc, new_sol, new_res, new_dir, got, put, isem, osem):
-    def fetch(k, ref):
-        return pltpu.make_async_copy(ref.at[:, 0, :], got.at[k], isem.at[k])
-
-    def store(k, ref):
-        return pltpu.make_async_copy(put.at[k], ref.at[:, 0, :], osem.at[k])
-
-    for k, ref in ((2, direc), (0, sol), (1, res)):
-        fetch(k, ref).start()
-    step, ratio = scal[:, 0:1], scal[:, 1:2]
-    fetch(2, direc).wait()
-    put[2] = comb[...] + ratio * got[2]
-    store(2, new_dir).start()
-    fetch(0, sol).wait()
-    put[0] = got[0] + step * got[2]
-    store(0, new_sol).start()
-    fetch(1, res).wait()
-    put[1] = got[1] - step * image[...]
-    store(1, new_res).start()
-    for k, ref in ((2, new_dir), (0, new_sol), (1, new_res)):
-        store(k, ref).wait()
+def finish(new_sol, new_res, new_dir, sol_out, res_out, dir_out, sem):
+    copies = [
+        pltpu.make_async_copy(src, dst.at[:, 0, :], sem.at[k])
+        for k, (src, dst) in enumerate(
+            ((new_sol, sol_out), (new_res, res_out), (new_dir, dir_out))
+        )
+    ]
+    for copy in copies:
+        copy.start()
+    for copy in copies:
+        copy.wait()
 
 
 def on_device(
@@ -521,20 +526,21 @@
     blocks = precond.shape[1]
     f32, bf16 = jnp.float32, jnp.bfloat16
     vmem = pl.BlockSpec(memory_space=pltpu.VMEM)
-    smem = pl.BlockSpec(memory_space=pltpu.SMEM)
     hbm = pl.BlockSpec(memory_space=pl.ANY)
-    V, D = pltpu.VMEM, lambda *k: pltpu.SemaphoreType.DMA(k)
-    vec = jax.ShapeDtypeStruct((rhs, share), f32)
-    image, comb, scal = pl.pallas_call(
+    V, S, D = pltpu.VMEM, pltpu.SMEM, lambda *k: pltpu.SemaphoreType.DMA(k)
+    vec = pltpu.VMEM((rhs, share), f32)
+    results = pl.pallas_call(
         functools.partial(kernel, T, O),
-        out_shape=[vec, vec, jax.ShapeDtypeStruct((rhs, 128), f32)],
-        in_specs=[hbm, vmem, vmem, smem, smem, smem, smem, vmem, hbm, hbm, hbm],
+        out_shape=[vec] * 3,
+        in_specs=[hbm] * 12,
         out_specs=[vmem] * 3,
         scratch_shapes=[
+            V((1, n), jnp.int32), V((1, n), jnp.int32), S((3, 4), f32), S((3, 4), f32),
+            S((3,), jnp.int32), S((3,), jnp.int32), V((1, share), f32),
             V((T, 3 * n, share), bf16), V((blocks, 128, 128), f32), V((rhs, share), f32),
-            V((rhs, share), f32), V((rhs, share), bf16), V((blocks, 128, 128), bf16),
+            V((rhs, share), f32), V((rhs, share), f32), V((rhs, share), bf16), V((blocks, 128, 128), bf16),
             V((blocks, 128, 128), bf16),
-            V((T - 1, rhs, share), bf16),
+            V((rhs, share), f32), V((T - 1, rhs, share), bf16),
             V((rhs, 3 * n), f32), V((O - 1, rhs, 3 * n), f32), V((T - 1, 1, n), jnp.int32),
             V((rhs // 2, n), f32), V((O - 1, rhs // 2, n), f32),
             V((rhs // 2, n), f32), V((T - 1, rhs // 2, n), f32), V((3, n, n), f32),
@@ -542,26 +548,31 @@
             V((T - 1, rhs, share), LINK), V((T - 1, rhs, share), LINK),
             V((rhs, share), f32), V((rhs, share), f32),
             V((1, 128), f32), V((T * O - 1, 1, 128), f32),
-            D(T), D(3), D(T - 1, CHUNKS), D(T - 1, CHUNKS), D(O - 1), D(O - 1),
+            D(T), D(11), D(T - 1, CHUNKS), D(T - 1, CHUNKS), D(O - 1), D(O - 1),
             D(T - 1), D(T - 1), D(O - 1), D(O - 1), D(T - 1), D(T - 1),
             D(T - 1, CHUNKS), D(T - 1, CHUNKS), D(T * O - 1), D(T * O - 1),
         ],
         compiler_params=pltpu.CompilerParams(
-            collective_id=0, has_side_effects=True, vmem_limit_bytes=56 * 1024 * 1024
+            collective_id=0, has_side_effects=True, vmem_limit_bytes=28 * 1024 * 1024
         ),
-    )(
-        design.reshape(3 * n, columns), segment_ids.reshape(1, n), gap_flags.reshape(1, n),
-        ar_roots, ma_roots, ar_order, ma_order, kaula, precond[0], residual, direction,
-    )
+    )(*[
+        pltpu.with_memory_space_constraint(v, pltpu.HBM)
+        for v in (
+            design.reshape(3 * n, columns), segment_ids.reshape(1, n), gap_flags.reshape(1, n),
+            ar_roots, ma_roots, ar_order, ma_order, kaula, precond[0], solution, residual,
+            direction,
+        )
+    ])
     full = jax.ShapeDtypeStruct(direction.shape, f32)
     return tuple(
         pl.pallas_call(
             finish,
             out_shape=[full] * 3,
-            in_specs=[vmem, vmem, vmem, hbm, hbm, hbm],
+            in_specs=[vmem] * 3,
             out_specs=[hbm] * 3,
-            scratch_shapes=[V((3, rhs, share), f32), V((3, rhs, share), f32), D(3), D(3)],
-        )(image, comb, scal, solution, residual, direction)
+            scratch_shapes=[D(3)],
+            compiler_params=pltpu.CompilerParams(vmem_limit_bytes=1024 * 1024),
+        )(*[pltpu.with_memory_space_constraint(v, pltpu.VMEM) for v in results])
     )
 
 

time: 46.8 us -> 43.3 us (0.925)
  Pallas kernels: 45.9 us -> 42.5 us
    pallas_call x2, Pallas kernels: 45.9 us -> 42.5 us  [the longest x1 41.7 us: on_device(): pl.pallas_call(functools.partial(kernel, T, O), out_shape=[vec] * 3, in_s...]
where the time goes in v3:
time: 43.3 us; the launch traced here: 43.1 us
  Pallas kernels  42.5 us (98%)
  between operations  0.64 us (1%)
    pallas_call x1, Pallas kernels, on_device(): pl.pallas_call(functools.partial(kernel, T, O), out_shape=[vec] * 3, in_s...  41.7 us

profile of v3, /device:TPU:0, one launch (start us, length us, event | category | flops | bytes accessed | tf_op | source)
XLA Modules:
  0.0 43.1 jit_solution(4592478332506633966)
XLA Ops:
  0.6 41.7 %shard_map.139 = (f32[16,2048]{1,0:T(8,128)S(1)}, f32[16,2048]{1,0:T(8,128)S(1)}, f32[16,2048]{1,0:T(8,128)S(1)}) custom-call(bf16[384,16384]{1,0:T(8,128)(2,1)} %bitcast.4, s32[1,128]{1,0:T(1,128)} %bitcast.6, s32[1,128]{1,0:T(1,128)} %bitcast.7, f32[3,4]{1,0:T(4,128)} %ar_hbm.1, f32[3,4]{1,0:T(4,128)} %ma_hbm.1, s32[3]{0:T(128)} %aro_hbm.1, s32[3]{0:T(128)} %mao_hbm.1, ...), custom_call_target="tpu_custom_call" | custom-call | tf_op jit(solution)/shard_map/pallas_call | solution.py:532
  42.3 0.8 %shard_map.140 = (f32[16,1,2048]{2,1,0:T(1,128)}, f32[16,1,2048]{2,1,0:T(1,128)}, f32[16,1,2048]{2,1,0:T(1,128)}) custom-call(f32[16,2048]{1,0:T(8,128)S(1)} %get-tuple-element.6.new_sol, f32[16,2048]{1,0:T(8,128)S(1)} %get-tuple-element.7.new_res, f32[16,2048]{1,0:T(8,128)S(1)} %get-tuple-element.8.new_dir), custom_call_target="tpu_custom_call" | custom-call | tf_op jit(solution)/shard_map/pallas_call | solution.py:568

commit v4 on v3

--- a/solution.py
+++ b/solution.py
@@ -10,6 +10,7 @@
 LINK = jnp.bfloat16
 LAGS = 4
 CHUNKS = 2
+APPLIED_AFTER = 5
 HI = lax.Precision.HIGHEST
 NN = (((1,), (0,)), ((), ()))
 NT = (((1,), (1,)), ((), ()))
@@ -174,10 +175,10 @@
     sol_in, res_in, direc_in,
     new_sol, new_res, new_dir,
     ids_in, gaps_in, ar_ref, ma_ref, aro_ref, mao_ref, kaula, dv, precond, sol, res, direc, packed, high, low_part,
-    image_out, got, obs_out, obs_in, ids_all, part_out, part_in, summ_out, summ_in, pt,
+    image_out, got, obs_out, obs_in, ids_all, summ_out, summ_in, pt,
     map_high, map_low, cross_high, cross_low, rs_out, rs_in, applied, image_applied,
     tot_out, tot_in,
-    dsem, in_sem, ga_s, ga_r, ob_s, ob_r, id_s, id_r, pa_s, pa_r, su_s, su_r,
+    dsem, in_sem, ga_s, ga_r, ob_s, ob_r, id_s, id_r, su_s, su_r,
     rs_s, rs_r, t1_s, t1_r,
 ):
     me, order = lax.axis_index("tm"), lax.axis_index("order")
@@ -187,8 +188,13 @@
     wide = share // CHUNKS
     bits = T.bit_length() - 1
 
-    def low(x):
-        return (x & -x).bit_length() - 1 if x else bits
+    levels = [(1 << b,) for b in reversed(range(2, bits))] + [(3, 2, 1)]
+
+    def level(x):
+        return max([i for i, offsets in enumerate(levels) if any(x & o for o in offsets)], default=-1)
+
+    def into(x):
+        return [o for offsets in levels[level(x) + 1 :] for o in offsets]
 
     def across(x):
         out = me
@@ -237,17 +243,16 @@
         ))
     ]
     barrier = pltpu.get_barrier_semaphore()
-    for b in range(bits):
+    for x in into(0):
         pl.semaphore_signal(
-            barrier, inc=1, device_id={"tm": across(1 << b)}, device_id_type=mesh_ids
+            barrier, inc=1, device_id={"tm": across(x)}, device_id_type=mesh_ids
         )
     for k in range(1, O):
         pl.semaphore_signal(barrier, inc=1, device_id=to_order(k), device_id_type=mesh_ids)
-    plan = [4, 2, 1, 6, 3, 5, 7] if T == 8 else sorted(range(1, T), key=lambda x: -low(x))
+    plan = sorted(range(1, T), key=lambda x: (level(x), x))
     for copy in get_small:
         copy.start()
-    load(0).start()
-    for x in plan:
+    for x in range(T):
         load(x).start()
     get_precond.start()
     get_res.start()
@@ -255,22 +260,22 @@
     get_direc.wait()
     packed[...] = direc[...].astype(jnp.bfloat16)
     get_small[0].wait()
-    pl.semaphore_wait(barrier, bits + O - 1)
+    pl.semaphore_wait(barrier, len(into(0)) + O - 1)
 
     id_copies, ga_copies = {}, {}
 
     def pass_on(x, c):
-        for b in reversed(range(low(x))):
-            to = x | 1 << b
+        for o in into(x):
+            to = x | o
             if c == 0:
                 id_copies[to] = remote(
                     ids_all.at[x - 1] if x else ids_in, ids_all.at[to - 1],
-                    id_s.at[to - 1], id_r.at[to - 1], {"tm": across(1 << b)},
+                    id_s.at[to - 1], id_r.at[to - 1], {"tm": across(o)},
                 )
                 id_copies[to].start()
             ga_copies[to, c] = remote(
                 (got.at[x - 1] if x else packed).at[:, cols(c)], got.at[to - 1, :, cols(c)],
-                ga_s.at[to - 1, c], ga_r.at[to - 1, c], {"tm": across(1 << b)},
+                ga_s.at[to - 1, c], ga_r.at[to - 1, c], {"tm": across(o)},
             )
             ga_copies[to, c].start()
 
@@ -285,8 +290,6 @@
 
     for copy in get_small[1:]:
         copy.wait()
-    load(0).wait()
-    obs = dot(packed[...], dv[0], NT)
     ids = ids_in[0:1, :].astype(jnp.float32)
     gaps3 = jnp.concatenate([gaps_in[0:1, :].astype(jnp.float32)] * 3, axis=1)
     building = filters(ar_ref, ma_ref, aro_ref, mao_ref, ids, pt)
@@ -313,34 +316,45 @@
         [dot(head_map[:, c * n : (c + 1) * n], pt[c], NT, HI) for c in range(3)], axis=1
     )
     both_maps = jnp.concatenate([tail_map, head_map], axis=0)
-    slots = jnp.concatenate([both_maps] * (n // 32), axis=0)
-    slot_row = lax.broadcasted_iota(jnp.int32, slots.shape, 0) // 32
-    top, rest = halves(jnp.where(slot_row == lax.rem(me, n // 32), slots, 0.0))
+    top, rest = halves(jnp.concatenate([both_maps] * 4, axis=0))
     map_high[...] = top
     map_low[...] = rest
-    steps = [("a", 4), ("a", 2), ("a", 1), ("o", 1), ("o", 4), ("a", 6), ("o", 2), ("o", 6),
-             ("b", 3), ("b", 5), ("b", 7)]
-    if T != 8:
-        steps = [("b", x) for x in plan]
-    for what, x in steps:
+    far = [x for x in plan if level(x) < len(levels) - 1]
+    near = [x for x in plan if level(x) == len(levels) - 1]
+    for x in far:
         for c in range(CHUNKS):
-            if what != "o":
+            arrive(x, c)
+    load(0).wait()
+    obs = dot(packed[...], dv[0], NT)
+    for x in near[:3] + far + near[3:]:
+        for c in range(CHUNKS):
+            if x in near:
                 arrive(x, c)
-            if what != "a":
-                obs = observe(x, c, obs)
-    half = rhs // 2
+            obs = observe(x, c, obs)
+    quarter = rhs // 4
     summary = dot3(obs * gaps3, map_high[...], map_low[...], NT)
-    part_out[...] = summary[:half] + pltpu.roll(summary[half:], n // 2, 1)
+    row = lax.broadcasted_iota(jnp.int32, summary.shape, 0)
+    lane = lax.broadcasted_iota(jnp.int32, summary.shape, 1)
+    turn = lax.rem(me, 4)
+    summary = jnp.where(lane // 32 == (row // quarter + turn) % 4, summary, 0.0)
+    summary = summary[: 2 * quarter] + summary[2 * quarter :]
+    summary = summary[:quarter] + summary[quarter:]
+    summ_out[...] = summary
+    summ_in[order * T + me] = summary
     obs_out[...] = obs
-    pa_copies = [
-        remote(part_out, part_in.at[k - 1], pa_s.at[k - 1], pa_r.at[k - 1], to_order(k))
-        for k in range(1, O)
-    ]
+    su_copies = []
+    for k in list(range(1, T)) + [0]:
+        for i in range(O):
+            if i or k:
+                at = i * T + k - 1
+                su_copies.append(
+                    remote(summ_out, summ_in.at[order * T + me], su_s.at[at], su_r.at[at], to_all(k, i))
+                )
     ob_copies = [
         remote(obs_out, obs_in.at[k - 1], ob_s.at[k - 1], ob_r.at[k - 1], to_order(k))
         for k in range(1, O)
     ]
-    for copy in pa_copies + ob_copies:
+    for copy in su_copies + ob_copies:
         copy.start()
 
     ids_e = []
@@ -362,15 +376,6 @@
     if direct:
         weights = state_weights(T, me, (16, n), links, throughs, fwd, bwd, energies)
 
-    for copy in pa_copies:
-        copy.wait_recv()
-    summ_out[...] = part_out[...] + sum([part_in[k] for k in range(1, O - 1)], part_in[0])
-    su_copies = [
-        remote(summ_out, summ_in.at[k - 1], su_s.at[k - 1], su_r.at[k - 1], to_tm(k))
-        for k in range(1, T)
-    ]
-    for copy in su_copies:
-        copy.start()
     if direct:
         top, rest = halves(dot(weights, tall(both_maps, n), NN, HI))
         cross_high[...] = top
@@ -387,26 +392,19 @@
         ],
         axis=1,
     )
-    get_precond.wait()
-    for m in range(blocks):
-        top, rest = halves(precond[m])
-        high[m] = top
-        low_part[m] = rest
-    get_res.wait()
-    applied[...] = preconditioned(res[...], slice(0, share))
     for copy in su_copies:
         copy.wait_recv()
-    folded = []
-    for e in range(T):
-        slot = jnp.minimum(lax.rem(me - e + T - 1, T), T - 2)
-        folded.append(jnp.where(me == e, summ_out[...], summ_in[slot]))
-    lane8 = lax.broadcasted_iota(jnp.int32, (half, n), 1)
+    slot = lax.broadcasted_iota(jnp.int32, (quarter, n), 1) // 32
+    sums = [sum([summ_in[i * T + e] for i in range(1, O)], summ_in[e]) for e in range(T)]
     groups = []
     for e in range(0, T, 4):
-        front, back = folded[e] + folded[e + 1], folded[e + 2] + folded[e + 3]
-        upper = jnp.where(lane8 < n // 2, front, back)
-        lower = pltpu.roll(jnp.where(lane8 < n // 2, back, front), n // 2, 1)
-        groups.append(jnp.concatenate([upper, lower], axis=0))
+        rows = []
+        for q in range(4):
+            picked = sums[e + (3 - q) % 4]
+            for at in range(3):
+                picked = jnp.where(slot == at, sums[e + (at - q) % 4], picked)
+            rows.append(pltpu.roll(picked, (n - 32 * q) % n, 1) if q else picked)
+        groups.append(jnp.concatenate(rows, axis=0))
     if direct:
         adjoint = local_back + dot3(
             jnp.concatenate(groups, axis=1), cross_high[...], cross_low[...], NN
@@ -442,19 +440,34 @@
         total = dot(weighted, dv[x, :, cols(c)], NN)
         if x == 0:
             total = total + kaula[:, cols(c)] * direc[:, cols(c)]
-        for b in range(low(x)):
-            rs_copies[x | 1 << b, c].wait_recv()
-            total = total + rs_in[(x | 1 << b) - 1, :, cols(c)].astype(jnp.float32)
+        for o in into(x):
+            rs_copies[x | o, c].wait_recv()
+            total = total + rs_in[(x | o) - 1, :, cols(c)].astype(jnp.float32)
         return total
 
-    for x in [7, 5, 3, 1, 6, 4, 2] if T == 8 else sorted(range(1, T), key=lambda x: (low(x), -x)):
+    def give_precond():
+        get_precond.wait()
+        for m in range(blocks):
+            top, rest = halves(precond[m])
+            high[m] = top
+            low_part[m] = rest
+        get_res.wait()
+        applied[...] = preconditioned(res[...], slice(0, share))
+
+    def last_offset(x):
+        return x & max(levels[level(x)])
+
+    outgoing = sorted(range(1, T), key=lambda x: (-level(x), -x))
+    for x in outgoing:
         for c in range(CHUNKS):
             rs_out[x - 1, :, cols(c)] = sum_of(x, c).astype(LINK)
             rs_copies[x, c] = remote(
                 rs_out.at[x - 1, :, cols(c)], rs_in.at[x - 1, :, cols(c)],
-                rs_s.at[x - 1, c], rs_r.at[x - 1, c], {"tm": across(1 << low(x))},
+                rs_s.at[x - 1, c], rs_r.at[x - 1, c], {"tm": across(last_offset(x))},
             )
             rs_copies[x, c].start()
+        if x == outgoing[APPLIED_AFTER]:
+            give_precond()
     for c in range(CHUNKS):
         piece = sum_of(0, c)
         image_out[:, cols(c)] = piece
@@ -498,7 +511,7 @@
     for copies in (id_copies, ga_copies, rs_copies):
         for copy in copies.values():
             copy.wait_send()
-    for copy in pa_copies + ob_copies + su_copies + tot_copies:
+    for copy in ob_copies + su_copies + tot_copies:
         copy.wait_send()
 
 
@@ -542,14 +555,13 @@
             V((blocks, 128, 128), bf16),
             V((rhs, share), f32), V((T - 1, rhs, share), bf16),
             V((rhs, 3 * n), f32), V((O - 1, rhs, 3 * n), f32), V((T - 1, 1, n), jnp.int32),
-            V((rhs // 2, n), f32), V((O - 1, rhs // 2, n), f32),
-            V((rhs // 2, n), f32), V((T - 1, rhs // 2, n), f32), V((3, n, n), f32),
+            V((rhs // 4, n), f32), V((T * O, rhs // 4, n), f32), V((3, n, n), f32),
             V((n, 3 * n), bf16), V((n, 3 * n), bf16), V((32 * T, 3 * n), bf16), V((32 * T, 3 * n), bf16),
             V((T - 1, rhs, share), LINK), V((T - 1, rhs, share), LINK),
             V((rhs, share), f32), V((rhs, share), f32),
             V((1, 128), f32), V((T * O - 1, 1, 128), f32),
             D(T), D(11), D(T - 1, CHUNKS), D(T - 1, CHUNKS), D(O - 1), D(O - 1),
-            D(T - 1), D(T - 1), D(O - 1), D(O - 1), D(T - 1), D(T - 1),
+            D(T - 1), D(T - 1), D(T * O - 1), D(T * O - 1),
             D(T - 1, CHUNKS), D(T - 1, CHUNKS), D(T * O - 1), D(T * O - 1),
         ],
         compiler_params=pltpu.CompilerParams(

time: 43.3 us -> 39.6 us (0.915)
  Pallas kernels: 42.5 us -> 38.8 us
    pallas_call x1, Pallas kernels: 41.7 us -> 38.1 us  [on_device(): pl.pallas_call(functools.partial(kernel, T, O), out_shape=[vec] * 3, in_s...]
where the time goes in v4:
time: 39.6 us; the launch traced here: 39.5 us
  Pallas kernels  38.8 us (98%)
  between operations  0.64 us (2%)
    pallas_call x1, Pallas kernels, on_device(): pl.pallas_call(functools.partial(kernel, T, O), out_shape=[vec] * 3, in_s...  38.1 us

profile of v4, /device:TPU:0, one launch (start us, length us, event | category | flops | bytes accessed | tf_op | source)
XLA Modules:
  0.0 39.5 jit_solution(10549169847563724324)
XLA Ops:
  0.6 38.1 %shard_map.139 = (f32[16,2048]{1,0:T(8,128)S(1)}, f32[16,2048]{1,0:T(8,128)S(1)}, f32[16,2048]{1,0:T(8,128)S(1)}) custom-call(bf16[384,16384]{1,0:T(8,128)(2,1)} %bitcast.4, s32[1,128]{1,0:T(1,128)} %bitcast.6, s32[1,128]{1,0:T(1,128)} %bitcast.7, f32[3,4]{1,0:T(4,128)} %ar_hbm.1, f32[3,4]{1,0:T(4,128)} %ma_hbm.1, s32[3]{0:T(128)} %aro_hbm.1, s32[3]{0:T(128)} %mao_hbm.1, ...), custom_call_target="tpu_custom_call" | custom-call | tf_op jit(solution)/shard_map/pallas_call | solution.py:545
  38.7 0.8 %shard_map.140 = (f32[16,1,2048]{2,1,0:T(1,128)}, f32[16,1,2048]{2,1,0:T(1,128)}, f32[16,1,2048]{2,1,0:T(1,128)}) custom-call(f32[16,2048]{1,0:T(8,128)S(1)} %get-tuple-element.6.new_sol, f32[16,2048]{1,0:T(8,128)S(1)} %get-tuple-element.7.new_res, f32[16,2048]{1,0:T(8,128)S(1)} %get-tuple-element.8.new_dir), custom_call_target="tpu_custom_call" | custom-call | tf_op jit(solution)/shard_map/pallas_call | solution.py:580

commit v5 on v4

--- a/solution.py
+++ b/solution.py
@@ -10,7 +10,6 @@
 LINK = jnp.bfloat16
 LAGS = 4
 CHUNKS = 2
-APPLIED_AFTER = 5
 HI = lax.Precision.HIGHEST
 NN = (((1,), (0,)), ((), ()))
 NT = (((1,), (1,)), ((), ()))
@@ -174,9 +173,9 @@
     design, ids_hbm, gaps_hbm, ar_hbm, ma_hbm, aro_hbm, mao_hbm, kaula_hbm, precond_in,
     sol_in, res_in, direc_in,
     new_sol, new_res, new_dir,
-    ids_in, gaps_in, ar_ref, ma_ref, aro_ref, mao_ref, kaula, dv, precond, sol, res, direc, packed, high, low_part,
-    image_out, got, obs_out, obs_in, ids_all, summ_out, summ_in, pt,
-    map_high, map_low, cross_high, cross_low, rs_out, rs_in, applied, image_applied,
+    ids_in, gaps_in, ar_ref, ma_ref, aro_ref, mao_ref, kaula, dv, precond, sol, res, direc, packed, split,
+    image_out, got, obs_out, obs_in, ids_all, summ_out, summ_in, pt, back_high, back_low, local_back,
+    map_high, map_low, cross_high, cross_low, rs_out, rs_in, parts, applied, image_applied,
     tot_out, tot_in,
     dsem, in_sem, ga_s, ga_r, ob_s, ob_r, id_s, id_r, su_s, su_r,
     rs_s, rs_r, t1_s, t1_r,
@@ -196,17 +195,23 @@
     def into(x):
         return [o for offsets in levels[level(x) + 1 :] for o in offsets]
 
-    def across(x):
+    def place(x):
         out = me
         for b in range(bits):
             if x >> b & 1:
                 out = out + (1 << b) * (1 - 2 * lax.rem(lax.div(me, 1 << b), 2))
         return out
 
+    places = [place(x) for x in range(T)]
+
+    def across(x):
+        return places[x]
+
     def cols(c):
         return slice(c * wide, (c + 1) * wide)
 
     mesh_ids = pl.DeviceIdType.MESH
+    apart = pl.when(me >= 0)
 
     def to_tm(k):
         return {"tm": lax.rem(me + k, T)}
@@ -264,18 +269,18 @@
 
     id_copies, ga_copies = {}, {}
 
-    def pass_on(x, c):
-        for o in into(x):
+    def pass_on(x, c, offsets):
+        for o in offsets:
             to = x | o
             if c == 0:
                 id_copies[to] = remote(
                     ids_all.at[x - 1] if x else ids_in, ids_all.at[to - 1],
-                    id_s.at[to - 1], id_r.at[to - 1], {"tm": across(o)},
+                    id_s, id_r.at[to - 1], {"tm": across(o)},
                 )
                 id_copies[to].start()
             ga_copies[to, c] = remote(
                 (got.at[x - 1] if x else packed).at[:, cols(c)], got.at[to - 1, :, cols(c)],
-                ga_s.at[to - 1, c], ga_r.at[to - 1, c], {"tm": across(o)},
+                ga_s, ga_r.at[to - 1, c], {"tm": across(o)},
             )
             ga_copies[to, c].start()
 
@@ -283,10 +288,11 @@
         if c == 0:
             id_copies[x].wait_recv()
         ga_copies[x, c].wait_recv()
-        pass_on(x, c)
-
-    for c in range(CHUNKS):
-        pass_on(0, c)
+        pass_on(x, c, into(x))
+
+    for o in into(0):
+        for c in range(CHUNKS):
+            pass_on(0, c, [o])
 
     for copy in get_small[1:]:
         copy.wait()
@@ -299,13 +305,19 @@
         out = []
         for m in range(at.start // 128, at.stop // 128):
             x = v[:, m * 128 - at.start : (m + 1) * 128 - at.start]
-            out.append(dot3(x, high[m], low_part[m], NT))
+            top, rest = halves(x)
+            both = dot(jnp.concatenate([top, rest], axis=0), split[m], NT)
+            out.append(both[:rhs, :128] + both[rhs:, :128] + both[:rhs, 128:])
         return jnp.concatenate(out, axis=1)
 
-    def observe(x, c, obs):
+    def observe(x, c, at):
         if c == 0:
             load(x).wait()
-        return obs + dot(got[x - 1, :, cols(c)], dv[x, :, cols(c)], NT)
+
+        @apart
+        def _():
+            for k in range(0, 3 * n, n):
+                obs_out[:, k : k + n] += dot(got[x - 1, :, at], dv[x, k : k + n, at], NT)
 
     next(building)
     ca, ab, fwd, bwd = next(building)
@@ -319,19 +331,27 @@
     top, rest = halves(jnp.concatenate([both_maps] * 4, axis=0))
     map_high[...] = top
     map_low[...] = rest
+    for c in range(3):
+        top, rest = halves(dot(pt[c], pt[c], NT, HI))
+        back_high[c] = top
+        back_low[c] = rest
+    load(0).wait()
+    obs_out[...] = dot(packed[...], dv[0], NT)
     far = [x for x in plan if level(x) < len(levels) - 1]
     near = [x for x in plan if level(x) == len(levels) - 1]
     for x in far:
         for c in range(CHUNKS):
             arrive(x, c)
-    load(0).wait()
-    obs = dot(packed[...], dv[0], NT)
     for x in near[:3] + far + near[3:]:
         for c in range(CHUNKS):
             if x in near:
                 arrive(x, c)
-            obs = observe(x, c, obs)
+            if x == T - 1:
+                observe(x, c, cols(c))
+        if x < T - 1:
+            observe(x, 0, slice(0, share))
     quarter = rhs // 4
+    obs = obs_out[...]
     summary = dot3(obs * gaps3, map_high[...], map_low[...], NT)
     row = lax.broadcasted_iota(jnp.int32, summary.shape, 0)
     lane = lax.broadcasted_iota(jnp.int32, summary.shape, 1)
@@ -341,59 +361,63 @@
     summary = summary[:quarter] + summary[quarter:]
     summ_out[...] = summary
     summ_in[order * T + me] = summary
-    obs_out[...] = obs
     su_copies = []
     for k in list(range(1, T)) + [0]:
         for i in range(O):
             if i or k:
-                at = i * T + k - 1
                 su_copies.append(
-                    remote(summ_out, summ_in.at[order * T + me], su_s.at[at], su_r.at[at], to_all(k, i))
+                    remote(summ_out, summ_in.at[order * T + me], su_s, su_r, to_all(k, i))
                 )
     ob_copies = [
-        remote(obs_out, obs_in.at[k - 1], ob_s.at[k - 1], ob_r.at[k - 1], to_order(k))
+        remote(obs_out, obs_in.at[k - 1], ob_s, ob_r, to_order(k))
         for k in range(1, O)
     ]
     for copy in su_copies + ob_copies:
         copy.start()
 
-    ids_e = []
-    for e in range(T):
-        v = ids
-        for x in range(1, T):
-            v = jnp.where(across(x) == e, ids_all[x - 1].astype(jnp.float32), v)
-        ids_e.append(v)
-    firsts = [v[:, 0:1] for v in ids_e]
-    lasts = [v[:, n - 1 : n] for v in ids_e]
-    runs = jnp.concatenate(
-        [ca * jnp.where(v == f, 1.0, 0.0) for v, f in zip(ids_e, firsts)], axis=0
-    )
-    energy = dot(runs, tall(ca, n), NT, HI)
-    energies = [bands(energy[16 * e : 16 * e + 16]) for e in range(T)]
-    links = [None] + [jnp.where(lasts[e - 1] == firsts[e], 1.0, 0.0) for e in range(1, T)]
-    throughs = [jnp.where(firsts[e] == lasts[e], 1.0, 0.0) for e in range(T)]
     direct = T <= 8
+
+    def ranges():
+        ids_e = []
+        for e in range(T):
+            v = ids
+            for x in range(1, T):
+                v = jnp.where(across(x) == e, ids_all[x - 1].astype(jnp.float32), v)
+            ids_e.append(v)
+        firsts = [v[:, 0:1] for v in ids_e]
+        lasts = [v[:, n - 1 : n] for v in ids_e]
+        runs = jnp.concatenate(
+            [ca * jnp.where(v == f, 1.0, 0.0) for v, f in zip(ids_e, firsts)], axis=0
+        )
+        energy = dot(runs, tall(ca, n), NT, HI)
+        energies = [bands(energy[16 * e : 16 * e + 16]) for e in range(T)]
+        links = [None] + [
+            jnp.where(lasts[e - 1] == firsts[e], 1.0, 0.0) for e in range(1, T)
+        ]
+        throughs = [jnp.where(firsts[e] == lasts[e], 1.0, 0.0) for e in range(T)]
+        return links, throughs, energies
+
     if direct:
-        weights = state_weights(T, me, (16, n), links, throughs, fwd, bwd, energies)
-
-    if direct:
-        top, rest = halves(dot(weights, tall(both_maps, n), NN, HI))
-        cross_high[...] = top
-        cross_low[...] = rest
-    for copy in ob_copies:
-        copy.wait_recv()
+        @apart
+        def _():
+            links, throughs, energies = ranges()
+            weights = state_weights(T, me, (16, n), links, throughs, fwd, bwd, energies)
+            top, rest = halves(dot(weights, tall(both_maps, n), NN, HI))
+            cross_high[...] = top
+            cross_low[...] = rest
+    else:
+        links, throughs, energies = ranges()
+    ob_all = remote(obs_in, obs_in, ob_s, ob_r, to_tm(1))
+    ob_all.wait_recv()
     for k in range(1, O):
         obs = obs + obs_in[k - 1]
     masked = obs * gaps3
-    local_back = jnp.concatenate(
-        [
-            dot(dot(masked[:, c * n : (c + 1) * n], pt[c], NN, HI), pt[c], NT, HI)
-            for c in range(3)
-        ],
-        axis=1,
-    )
-    for copy in su_copies:
-        copy.wait_recv()
+    for c in range(3):
+        at = slice(c * n, (c + 1) * n)
+        local_back[:, at] = dot3(masked[:, at], back_high[c], back_low[c], NN)
+    others = summ_in.at[pl.ds(1, T * O - 1)]
+    su_all = remote(others, others, su_s, su_r, to_tm(1))
+    su_all.wait_recv()
     slot = lax.broadcasted_iota(jnp.int32, (quarter, n), 1) // 32
     sums = [sum([summ_in[i * T + e] for i in range(1, O)], summ_in[e]) for e in range(T)]
     groups = []
@@ -406,7 +430,7 @@
             rows.append(pltpu.roll(picked, (n - 32 * q) % n, 1) if q else picked)
         groups.append(jnp.concatenate(rows, axis=0))
     if direct:
-        adjoint = local_back + dot3(
+        adjoint = local_back[...] + dot3(
             jnp.concatenate(groups, axis=1), cross_high[...], cross_low[...], NN
         )
     else:
@@ -431,15 +455,16 @@
             back = back * links[e]
             mine_back = jnp.where(me == e - 1, back, mine_back)
         states = mine_back + pltpu.roll(mine_in, 16, 1)
-        adjoint = local_back + dot(states, tall(both_maps, n), NN, HI)
+        adjoint = local_back[...] + dot(states, tall(both_maps, n), NN, HI)
     weighted = (adjoint * gaps3).astype(jnp.bfloat16)
 
     rs_copies = {}
 
+    def part(x):
+        return dot(weighted, dv[x], NN)
+
     def sum_of(x, c):
-        total = dot(weighted, dv[x, :, cols(c)], NN)
-        if x == 0:
-            total = total + kaula[:, cols(c)] * direc[:, cols(c)]
+        total = parts[([0] + far).index(x), :, cols(c)]
         for o in into(x):
             rs_copies[x | o, c].wait_recv()
             total = total + rs_in[(x | o) - 1, :, cols(c)].astype(jnp.float32)
@@ -449,25 +474,38 @@
         get_precond.wait()
         for m in range(blocks):
             top, rest = halves(precond[m])
-            high[m] = top
-            low_part[m] = rest
+            split[m, :128] = top
+            split[m, 128:] = rest
         get_res.wait()
         applied[...] = preconditioned(res[...], slice(0, share))
 
     def last_offset(x):
         return x & max(levels[level(x)])
 
-    outgoing = sorted(range(1, T), key=lambda x: (-level(x), -x))
-    for x in outgoing:
+    def send(x, c):
+        rs_copies[x, c] = remote(
+            rs_out.at[x - 1, :, cols(c)], rs_in.at[x - 1, :, cols(c)],
+            rs_s, rs_r.at[x - 1, c], {"tm": across(last_offset(x))},
+        )
+        rs_copies[x, c].start()
+
+    leaves = [x for x in reversed(plan) if level(x) == len(levels) - 1]
+    for x in [x for x in leaves if x > 3] + [3, 2, 1]:
+        @apart
+        def _(x=x):
+            rs_out[x - 1] = part(x).astype(LINK)
+        for c in range(CHUNKS):
+            send(x, c)
+    @apart
+    def _():
+        for x in far:
+            parts[1 + far.index(x)] = part(x)
+        parts[0] = part(0) + kaula[...] * direc[...]
+    give_precond()
+    for x in reversed(far):
         for c in range(CHUNKS):
             rs_out[x - 1, :, cols(c)] = sum_of(x, c).astype(LINK)
-            rs_copies[x, c] = remote(
-                rs_out.at[x - 1, :, cols(c)], rs_in.at[x - 1, :, cols(c)],
-                rs_s.at[x - 1, c], rs_r.at[x - 1, c], {"tm": across(last_offset(x))},
-            )
-            rs_copies[x, c].start()
-        if x == outgoing[APPLIED_AFTER]:
-            give_precond()
+            send(x, c)
     for c in range(CHUNKS):
         piece = sum_of(0, c)
         image_out[:, cols(c)] = piece
@@ -490,13 +528,11 @@
         for k in range(T):
             if i or k:
                 at = i * T + k - 1
-                tot_copies.append(
-                    remote(tot_out, tot_in.at[at], t1_s.at[at], t1_r.at[at], to_all(k, i))
-                )
+                tot_copies.append(remote(tot_out, tot_in.at[at], t1_s, t1_r, to_all(k, i)))
     for copy in tot_copies:
         copy.start()
-    for copy in tot_copies:
-        copy.wait_recv()
+    tot_all = remote(tot_in, tot_in, t1_s, t1_r, to_tm(1))
+    tot_all.wait_recv()
     total = total + jnp.sum(tot_in[...], axis=0)
     wide = jnp.broadcast_to(total[0:1, :], (rhs, 128))
     old_rz, curvature, cross, quad = [
@@ -508,10 +544,10 @@
     new_sol[...] = sol[...] + step * d
     new_res[...] = r - step * image
     new_dir[...] = app - step * imapp + (new_rz / old_rz) * d
-    for copies in (id_copies, ga_copies, rs_copies):
-        for copy in copies.values():
-            copy.wait_send()
-    for copy in ob_copies + su_copies + tot_copies:
+    sent = [(ids_all, id_s, id_r.at[0]), (got, ga_s, ga_r.at[0, 0]), (rs_out, rs_s, rs_r.at[0, 0])]
+    for ref, out, back in sent:
+        remote(ref, ref, out, back, to_tm(1)).wait_send()
+    for copy in (su_all, ob_all, tot_all):
         copy.wait_send()
 
 
@@ -540,7 +576,7 @@
     f32, bf16 = jnp.float32, jnp.bfloat16
     vmem = pl.BlockSpec(memory_space=pltpu.VMEM)
     hbm = pl.BlockSpec(memory_space=pl.ANY)
-    V, S, D = pltpu.VMEM, pltpu.SMEM, lambda *k: pltpu.SemaphoreType.DMA(k)
+    V, S, D = pltpu.VMEM, pltpu.SMEM, lambda *k: pltpu.SemaphoreType.DMA(k) if k else pltpu.SemaphoreType.DMA
     vec = pltpu.VMEM((rhs, share), f32)
     results = pl.pallas_call(
         functools.partial(kernel, T, O),
@@ -551,18 +587,18 @@
             V((1, n), jnp.int32), V((1, n), jnp.int32), S((3, 4), f32), S((3, 4), f32),
             S((3,), jnp.int32), S((3,), jnp.int32), V((1, share), f32),
             V((T, 3 * n, share), bf16), V((blocks, 128, 128), f32), V((rhs, share), f32),
-            V((rhs, share), f32), V((rhs, share), f32), V((rhs, share), bf16), V((blocks, 128, 128), bf16),
-            V((blocks, 128, 128), bf16),
+            V((rhs, share), f32), V((rhs, share), f32), V((rhs, share), bf16), V((blocks, 256, 128), bf16),
             V((rhs, share), f32), V((T - 1, rhs, share), bf16),
             V((rhs, 3 * n), f32), V((O - 1, rhs, 3 * n), f32), V((T - 1, 1, n), jnp.int32),
-            V((rhs // 4, n), f32), V((T * O, rhs // 4, n), f32), V((3, n, n), f32),
+            V((rhs // 4, n), f32), V((T * O, rhs // 4, n), f32), V((3, n, n), f32), V((3, n, n), bf16), V((3, n, n), bf16),
+            V((rhs, 3 * n), f32),
             V((n, 3 * n), bf16), V((n, 3 * n), bf16), V((32 * T, 3 * n), bf16), V((32 * T, 3 * n), bf16),
             V((T - 1, rhs, share), LINK), V((T - 1, rhs, share), LINK),
+            V((max(T // 4, 1), rhs, share), f32),
             V((rhs, share), f32), V((rhs, share), f32),
             V((1, 128), f32), V((T * O - 1, 1, 128), f32),
-            D(T), D(11), D(T - 1, CHUNKS), D(T - 1, CHUNKS), D(O - 1), D(O - 1),
-            D(T - 1), D(T - 1), D(T * O - 1), D(T * O - 1),
-            D(T - 1, CHUNKS), D(T - 1, CHUNKS), D(T * O - 1), D(T * O - 1),
+            D(T), D(11), D(), D(T - 1, CHUNKS), D(), D(), D(), D(T - 1), D(), D(),
+            D(), D(T - 1, CHUNKS), D(), D(),
         ],
         compiler_params=pltpu.CompilerParams(
             collective_id=0, has_side_effects=True, vmem_limit_bytes=28 * 1024 * 1024

time: 39.6 us -> 38.5 us (0.972)
  Pallas kernels: 38.8 us -> 37.7 us
    pallas_call x1, Pallas kernels: 38.1 us -> 37 us  [on_device(): pl.pallas_call(functools.partial(kernel, T, O), out_shape=[vec] * 3, in_s...]
where the time goes in v5:
time: 38.5 us; the launch traced here: 38.4 us
  Pallas kernels  37.7 us (98%)
  between operations  0.64 us (2%)
    pallas_call x1, Pallas kernels, on_device(): pl.pallas_call(functools.partial(kernel, T, O), out_shape=[vec] * 3, in_s...  37 us
    pallas_call x1, Pallas kernels, on_device(): pl.pallas_call(finish, out_shape=[full] * 3, in_specs=[vmem] * 3, out_spe...  0.77 us

profile of v5, /device:TPU:0, one launch (start us, length us, event | category | flops | bytes accessed | tf_op | source)
XLA Modules:
  0.0 38.4 jit_solution(7295914016793180777)
XLA Ops:
  0.6 37.0 %shard_map.139 = (f32[16,2048]{1,0:T(8,128)S(1)}, f32[16,2048]{1,0:T(8,128)S(1)}, f32[16,2048]{1,0:T(8,128)S(1)}) custom-call(bf16[384,16384]{1,0:T(8,128)(2,1)} %bitcast.4, s32[1,128]{1,0:T(1,128)} %bitcast.6, s32[1,128]{1,0:T(1,128)} %bitcast.7, f32[3,4]{1,0:T(4,128)} %ar_hbm.1, f32[3,4]{1,0:T(4,128)} %ma_hbm.1, s32[3]{0:T(128)} %aro_hbm.1, s32[3]{0:T(128)} %mao_hbm.1, ...), custom_call_target="tpu_custom_call" | custom-call | tf_op jit(solution)/shard_map/pallas_call | solution.py:581
  37.6 0.8 %shard_map.140 = (f32[16,1,2048]{2,1,0:T(1,128)}, f32[16,1,2048]{2,1,0:T(1,128)}, f32[16,1,2048]{2,1,0:T(1,128)}) custom-call(f32[16,2048]{1,0:T(8,128)S(1)} %get-tuple-element.6.new_sol, f32[16,2048]{1,0:T(8,128)S(1)} %get-tuple-element.7.new_res, f32[16,2048]{1,0:T(8,128)S(1)} %get-tuple-element.8.new_dir), custom_call_target="tpu_custom_call" | custom-call | tf_op jit(solution)/shard_map/pallas_call | solution.py:616

commit v6 on v5

--- a/solution.py
+++ b/solution.py
@@ -175,7 +175,7 @@
     new_sol, new_res, new_dir,
     ids_in, gaps_in, ar_ref, ma_ref, aro_ref, mao_ref, kaula, dv, precond, sol, res, direc, packed, split,
     image_out, got, obs_out, obs_in, ids_all, summ_out, summ_in, pt, back_high, back_low, local_back,
-    map_high, map_low, cross_high, cross_low, rs_out, rs_in, parts, applied, image_applied,
+    map_high, map_low, cross_high, cross_low, rs_out, rs_in, parts, first_sum, applied, image_applied,
     tot_out, tot_in,
     dsem, in_sem, ga_s, ga_r, ob_s, ob_r, id_s, id_r, su_s, su_r,
     rs_s, rs_r, t1_s, t1_r,
@@ -294,10 +294,9 @@
         for c in range(CHUNKS):
             pass_on(0, c, [o])
 
-    for copy in get_small[1:]:
+    for copy in get_small[1:5]:
         copy.wait()
     ids = ids_in[0:1, :].astype(jnp.float32)
-    gaps3 = jnp.concatenate([gaps_in[0:1, :].astype(jnp.float32)] * 3, axis=1)
     building = filters(ar_ref, ma_ref, aro_ref, mao_ref, ids, pt)
     next(building)
 
@@ -351,6 +350,9 @@
         if x < T - 1:
             observe(x, 0, slice(0, share))
     quarter = rhs // 4
+    for copy in get_small[5:]:
+        copy.wait()
+    gaps3 = jnp.concatenate([gaps_in[0:1, :].astype(jnp.float32)] * 3, axis=1)
     obs = obs_out[...]
     summary = dot3(obs * gaps3, map_high[...], map_low[...], NT)
     row = lax.broadcasted_iota(jnp.int32, summary.shape, 0)
@@ -470,6 +472,9 @@
             total = total + rs_in[(x | o) - 1, :, cols(c)].astype(jnp.float32)
         return total
 
+    def narrow(v):
+        return sum([v[:, k : k + 128] for k in range(128, v.shape[1], 128)], v[:, :128])
+
     def give_precond():
         get_precond.wait()
         for m in range(blocks):
@@ -477,7 +482,9 @@
             split[m, :128] = top
             split[m, 128:] = rest
         get_res.wait()
-        applied[...] = preconditioned(res[...], slice(0, share))
+        known = preconditioned(res[...], slice(0, share))
+        applied[...] = known
+        first_sum[...] = narrow(res[...] * known)
 
     def last_offset(x):
         return x & max(levels[level(x)])
@@ -490,7 +497,7 @@
         rs_copies[x, c].start()
 
     leaves = [x for x in reversed(plan) if level(x) == len(levels) - 1]
-    for x in [x for x in leaves if x > 3] + [3, 2, 1]:
+    for x in [x for x in leaves if x > 3]:
         @apart
         def _(x=x):
             rs_out[x - 1] = part(x).astype(LINK)
@@ -502,26 +509,32 @@
             parts[1 + far.index(x)] = part(x)
         parts[0] = part(0) + kaula[...] * direc[...]
     give_precond()
+    for x in (3, 2, 1):
+        @apart
+        def _(x=x):
+            rs_out[x - 1] = part(x).astype(LINK)
+        for c in range(CHUNKS):
+            send(x, c)
     for x in reversed(far):
         for c in range(CHUNKS):
             rs_out[x - 1, :, cols(c)] = sum_of(x, c).astype(LINK)
             send(x, c)
+    inner_sums = [first_sum[...]] + [jnp.zeros((rhs, 128), jnp.float32)] * 3
+    get_sol.wait()
     for c in range(CHUNKS):
         piece = sum_of(0, c)
         image_out[:, cols(c)] = piece
-        image_applied[:, cols(c)] = preconditioned(piece, cols(c))
-    image = image_out[...]
-    get_sol.wait()
-    app, imapp = applied[...], image_applied[...]
-    d, r = direc[...], res[...]
+        moved = preconditioned(piece, cols(c))
+        image_applied[:, cols(c)] = moved
+        known = applied[:, cols(c)]
+        for q, product in enumerate((direc[:, cols(c)] * piece, piece * known, piece * moved)):
+            inner_sums[q + 1] += narrow(product)
     lane = lax.broadcasted_iota(jnp.int32, (rhs, 128), 1)
     row = lax.broadcasted_iota(jnp.int32, (rhs, 128), 0)
-    products = [r * app, d * image, image * app, image * imapp]
     total = jnp.zeros((rhs, 128), jnp.float32)
-    for q, product in enumerate(products):
+    for q, product in enumerate(inner_sums):
         total = jnp.where(lane == q * rhs + row, jnp.sum(product, axis=1, keepdims=True), total)
     total = jnp.sum(total, axis=0, keepdims=True)
-
     tot_out[...] = total
     tot_copies = []
     for i in range(O):
@@ -541,6 +554,8 @@
     ]
     step = old_rz / curvature
     new_rz = old_rz - 2.0 * step * cross + step * step * quad
+    app, imapp, image = applied[...], image_applied[...], image_out[...]
+    d, r = direc[...], res[...]
     new_sol[...] = sol[...] + step * d
     new_res[...] = r - step * image
     new_dir[...] = app - step * imapp + (new_rz / old_rz) * d
@@ -594,7 +609,7 @@
             V((rhs, 3 * n), f32),
             V((n, 3 * n), bf16), V((n, 3 * n), bf16), V((32 * T, 3 * n), bf16), V((32 * T, 3 * n), bf16),
             V((T - 1, rhs, share), LINK), V((T - 1, rhs, share), LINK),
-            V((max(T // 4, 1), rhs, share), f32),
+            V((max(T // 4, 1), rhs, share), f32), V((rhs, 128), f32),
             V((rhs, share), f32), V((rhs, share), f32),
             V((1, 128), f32), V((T * O - 1, 1, 128), f32),
             D(T), D(11), D(), D(T - 1, CHUNKS), D(), D(), D(), D(T - 1), D(), D(),

time: 38.5 us -> 37.6 us (0.977)
  Pallas kernels: 37.7 us -> 36.8 us
    pallas_call x1, Pallas kernels: 37 us -> 36.1 us  [on_device(): pl.pallas_call(functools.partial(kernel, T, O), out_shape=[vec] * 3, in_s...]
where the time goes in v6:
time: 37.6 us; the launch traced here: 37.5 us
  Pallas kernels  36.8 us (98%)
  between operations  0.64 us (2%)
    pallas_call x1, Pallas kernels, on_device(): pl.pallas_call(functools.partial(kernel, T, O), out_shape=[vec] * 3, in_s...  36.1 us
    pallas_call x1, Pallas kernels, on_device(): pl.pallas_call(finish, out_shape=[full] * 3, in_specs=[vmem] * 3, out_spe...  0.77 us

profile of v6, /device:TPU:0, one launch (start us, length us, event | category | flops | bytes accessed | tf_op | source)
XLA Modules:
  0.0 37.5 jit_solution(5799522033022893743)
XLA Ops:
  0.6 36.1 %shard_map.139 = (f32[16,2048]{1,0:T(8,128)S(1)}, f32[16,2048]{1,0:T(8,128)S(1)}, f32[16,2048]{1,0:T(8,128)S(1)}) custom-call(bf16[384,16384]{1,0:T(8,128)(2,1)} %bitcast.4, s32[1,128]{1,0:T(1,128)} %bitcast.6, s32[1,128]{1,0:T(1,128)} %bitcast.7, f32[3,4]{1,0:T(4,128)} %ar_hbm.1, f32[3,4]{1,0:T(4,128)} %ma_hbm.1, s32[3]{0:T(128)} %aro_hbm.1, s32[3]{0:T(128)} %mao_hbm.1, ...), custom_call_target="tpu_custom_call" | custom-call | tf_op jit(solution)/shard_map/pallas_call | solution.py:596
  36.7 0.8 %shard_map.140 = (f32[16,1,2048]{2,1,0:T(1,128)}, f32[16,1,2048]{2,1,0:T(1,128)}, f32[16,1,2048]{2,1,0:T(1,128)}) custom-call(f32[16,2048]{1,0:T(8,128)S(1)} %get-tuple-element.6.new_sol, f32[16,2048]{1,0:T(8,128)S(1)} %get-tuple-element.7.new_res, f32[16,2048]{1,0:T(8,128)S(1)} %get-tuple-element.8.new_dir), custom_call_target="tpu_custom_call" | custom-call | tf_op jit(solution)/shard_map/pallas_call | solution.py:631

commit v7 on v6

--- a/solution.py
+++ b/solution.py
@@ -467,9 +467,10 @@
 
     def sum_of(x, c):
         total = parts[([0] + far).index(x), :, cols(c)]
-        for o in into(x):
-            rs_copies[x | o, c].wait_recv()
-            total = total + rs_in[(x | o) - 1, :, cols(c)].astype(jnp.float32)
+        for y in reversed(range(1, T)):
+            if y ^ back_over(y) == x:
+                rs_copies[y, c].wait_recv()
+                total = total + rs_in[y - 1, :, cols(c)].astype(jnp.float32)
         return total
 
     def narrow(v):
@@ -486,18 +487,18 @@
         applied[...] = known
         first_sum[...] = narrow(res[...] * known)
 
-    def last_offset(x):
-        return x & max(levels[level(x)])
+    def back_over(x):
+        return x if x & 3 == 3 else x & max(levels[level(x)])
 
     def send(x, c):
         rs_copies[x, c] = remote(
             rs_out.at[x - 1, :, cols(c)], rs_in.at[x - 1, :, cols(c)],
-            rs_s, rs_r.at[x - 1, c], {"tm": across(last_offset(x))},
+            rs_s, rs_r.at[x - 1, c], {"tm": across(back_over(x))},
         )
         rs_copies[x, c].start()
 
     leaves = [x for x in reversed(plan) if level(x) == len(levels) - 1]
-    for x in [x for x in leaves if x > 3]:
+    for x in [x for x in leaves if x > 3 and x & 3 < 3]:
         @apart
         def _(x=x):
             rs_out[x - 1] = part(x).astype(LINK)
@@ -509,7 +510,7 @@
             parts[1 + far.index(x)] = part(x)
         parts[0] = part(0) + kaula[...] * direc[...]
     give_precond()
-    for x in (3, 2, 1):
+    for x in [x for x in leaves if x & 3 == 3] + [2, 1]:
         @apart
         def _(x=x):
             rs_out[x - 1] = part(x).astype(LINK)

time: 37.6 us -> 36.7 us (0.976)
  Pallas kernels: 36.8 us -> 35.9 us
    pallas_call x1, Pallas kernels: 36.1 us -> 35.1 us  [on_device(): pl.pallas_call(functools.partial(kernel, T, O), out_shape=[vec] * 3, in_s...]
where the time goes in v7:
time: 36.7 us; the launch traced here: 36.5 us
  Pallas kernels  35.9 us (98%)
  between operations  0.64 us (2%)
    pallas_call x1, Pallas kernels, on_device(): pl.pallas_call(functools.partial(kernel, T, O), out_shape=[vec] * 3, in_s...  35.1 us
    pallas_call x1, Pallas kernels, on_device(): pl.pallas_call(finish, out_shape=[full] * 3, in_specs=[vmem] * 3, out_spe...  0.77 us

profile of v7, /device:TPU:0, one launch (start us, length us, event | category | flops | bytes accessed | tf_op | source)
XLA Modules:
  0.0 36.5 jit_solution(15092554848289792465)
XLA Ops:
  0.6 35.1 %shard_map.139 = (f32[16,2048]{1,0:T(8,128)S(1)}, f32[16,2048]{1,0:T(8,128)S(1)}, f32[16,2048]{1,0:T(8,128)S(1)}) custom-call(bf16[384,16384]{1,0:T(8,128)(2,1)} %bitcast.4, s32[1,128]{1,0:T(1,128)} %bitcast.6, s32[1,128]{1,0:T(1,128)} %bitcast.7, f32[3,4]{1,0:T(4,128)} %ar_hbm.1, f32[3,4]{1,0:T(4,128)} %ma_hbm.1, s32[3]{0:T(128)} %aro_hbm.1, s32[3]{0:T(128)} %mao_hbm.1, ...), custom_call_target="tpu_custom_call" | custom-call | tf_op jit(solution)/shard_map/pallas_call | solution.py:597
  35.8 0.8 %shard_map.140 = (f32[16,1,2048]{2,1,0:T(1,128)}, f32[16,1,2048]{2,1,0:T(1,128)}, f32[16,1,2048]{2,1,0:T(1,128)}) custom-call(f32[16,2048]{1,0:T(8,128)S(1)} %get-tuple-element.6.new_sol, f32[16,2048]{1,0:T(8,128)S(1)} %get-tuple-element.7.new_res, f32[16,2048]{1,0:T(8,128)S(1)} %get-tuple-element.8.new_dir), custom_call_target="tpu_custom_call" | custom-call | tf_op jit(solution)/shard_map/pallas_call | solution.py:632

commit v8 on v7

--- a/solution.py
+++ b/solution.py
@@ -184,7 +184,7 @@
     rhs, share = packed.shape
     n = ids_in.shape[1]
     blocks = precond.shape[0]
-    wide = share // CHUNKS
+    bounds = [0, max(128, share * 10 // 16 // 128 * 128), share]
     bits = T.bit_length() - 1
 
     levels = [(1 << b,) for b in reversed(range(2, bits))] + [(3, 2, 1)]
@@ -208,7 +208,7 @@
         return places[x]
 
     def cols(c):
-        return slice(c * wide, (c + 1) * wide)
+        return slice(bounds[c], bounds[c + 1])
 
     mesh_ids = pl.DeviceIdType.MESH
     apart = pl.when(me >= 0)
@@ -509,7 +509,6 @@
         for x in far:
             parts[1 + far.index(x)] = part(x)
         parts[0] = part(0) + kaula[...] * direc[...]
-    give_precond()
     for x in [x for x in leaves if x & 3 == 3] + [2, 1]:
         @apart
         def _(x=x):
@@ -520,6 +519,7 @@
         for c in range(CHUNKS):
             rs_out[x - 1, :, cols(c)] = sum_of(x, c).astype(LINK)
             send(x, c)
+    give_precond()
     inner_sums = [first_sum[...]] + [jnp.zeros((rhs, 128), jnp.float32)] * 3
     get_sol.wait()
     for c in range(CHUNKS):

time: 36.7 us -> 37.6 us (1.025)
  Pallas kernels: 35.9 us -> 36.8 us
    pallas_call x1, Pallas kernels: 35.1 us -> 36.1 us  [on_device(): pl.pallas_call(functools.partial(kernel, T, O), out_shape=[vec] * 3, in_s...]
where the time goes in v8:
time: 37.6 us; the launch traced here: 37.5 us
  Pallas kernels  36.8 us (98%)
  between operations  0.64 us (2%)
    pallas_call x1, Pallas kernels, on_device(): pl.pallas_call(functools.partial(kernel, T, O), out_shape=[vec] * 3, in_s...  36.1 us
    pallas_call x1, Pallas kernels, on_device(): pl.pallas_call(finish, out_shape=[full] * 3, in_specs=[vmem] * 3, out_spe...  0.77 us

profile of v8, /device:TPU:0, one launch (start us, length us, event | category | flops | bytes accessed | tf_op | source)
XLA Modules:
  0.0 37.5 jit_solution(9135468136666216259)
XLA Ops:
  0.6 36.1 %shard_map.139 = (f32[16,2048]{1,0:T(8,128)S(1)}, f32[16,2048]{1,0:T(8,128)S(1)}, f32[16,2048]{1,0:T(8,128)S(1)}) custom-call(bf16[384,16384]{1,0:T(8,128)(2,1)} %bitcast.4, s32[1,128]{1,0:T(1,128)} %bitcast.6, s32[1,128]{1,0:T(1,128)} %bitcast.7, f32[3,4]{1,0:T(4,128)} %ar_hbm.1, f32[3,4]{1,0:T(4,128)} %ma_hbm.1, s32[3]{0:T(128)} %aro_hbm.1, s32[3]{0:T(128)} %mao_hbm.1, ...), custom_call_target="tpu_custom_call" | custom-call | tf_op jit(solution)/shard_map/pallas_call | solution.py:597
  36.7 0.8 %shard_map.140 = (f32[16,1,2048]{2,1,0:T(1,128)}, f32[16,1,2048]{2,1,0:T(1,128)}, f32[16,1,2048]{2,1,0:T(1,128)}) custom-call(f32[16,2048]{1,0:T(8,128)S(1)} %get-tuple-element.6.new_sol, f32[16,2048]{1,0:T(8,128)S(1)} %get-tuple-element.7.new_res, f32[16,2048]{1,0:T(8,128)S(1)} %get-tuple-element.8.new_dir), custom_call_target="tpu_custom_call" | custom-call | tf_op jit(solution)/shard_map/pallas_call | solution.py:632
